TPU v7x, 128 devices: a whole 4x4x4 slice. The times are simulated.
128 devices in a mesh: sub: 4 (over y), tm: 32 (over z, x, core).
Axes of the slice: x: 4, y: 4, z: 4, core: 2. Of those that a mesh axis runs over, the one named last changes fastest.
Arguments:
- streams: bfloat16 [2, 2160, 131072], P(None, 'sub', 'tm'), may hold values from -6 to 6
- beam_weights: bfloat16 [2, 100, 2160], P(None, None, 'sub'), may hold values from -0.09375 to 0.09375
- code_signs: int32 [32, 16], replicated, may hold values from 0 to 1
- gate_map: int32 [256], replicated, may hold values from 0 to 127, as said below
Outputs:
- profiles: float32 [128, 100, 128], P('tm', 'sub')
Inputs may be any that keep to these rules, and one draw needn't show every extreme that they name: `gate_map`: each range gate is named by exactly 2 sections.
All inputs are finite; a program needn't handle non-finite values.
Results may differ from a plain program's by a relative error of at most 0.0041.
Values may be sent and summed in bfloat16 or wider, within the bound.
A program may use at most 128 MiB of HBM per device.

v0:
```python
import math

import jax
import jax.numpy as jnp
from jax import lax
from jax.sharding import PartitionSpec as P

PKT = 32
IPP_LEN = 512
LAGS = 64
NCODES = 32
NBAUD = 16
BAUD_LEN = 8
SEC_LEN = 2
GATES = 128
NSEC = 256


def from_next(block, axis, distance):
    count = lax.axis_size(axis)
    return lax.ppermute(block, axis, [((i + distance) % count, i) for i in range(count)])


def form_beams(streams, beam_weights):
    subs = lax.axis_size("sub")
    w_real = beam_weights[0]
    w_imag = beam_weights[1]
    on_real = jnp.stack([w_real, w_imag], 1).reshape(-1, w_real.shape[1])
    on_imag = jnp.stack([-w_imag, w_real], 1).reshape(-1, w_real.shape[1])
    product = jnp.dot(on_real, streams[0], preferred_element_type=jnp.float32) + jnp.dot(
        on_imag, streams[1], preferred_element_type=jnp.float32
    )
    parts = product.reshape(subs, -1, streams.shape[2])
    arrived = lax.all_to_all(parts, "sub", split_axis=0, concat_axis=0, tiled=True)
    return arrived.sum(axis=0).astype(jnp.bfloat16)


def body(streams, beam_weights, code_signs, gate_map):
    tms = lax.axis_size("tm")
    here = lax.axis_index("tm")
    early = form_beams(streams, beam_weights)
    beams_here = early.shape[0] // 2
    chunks = early.shape[1] // PKT
    held = early.reshape(beams_here, 2, chunks, PKT)
    pieces = [held]
    for distance in (1, 2):
        later = from_next(held, "tm", distance)
        moved = jnp.concatenate([later[:, :, 1:], jnp.zeros_like(later[:, :, :1])], 2)
        pieces.append(jnp.where(here + distance >= tms, moved, later))
    wide = jnp.concatenate(pieces, 3)
    width = wide.shape[3]
    groups = IPP_LEN // PKT
    codes = (jnp.arange(chunks) * (tms * PKT // IPP_LEN) + here // groups) % NCODES
    bauds = (here * (PKT // BAUD_LEN) + jnp.arange(width) // BAUD_LEN) % NBAUD
    signs = (2 * code_signs - 1)[codes][:, bauds].astype(jnp.bfloat16)
    coded = wide * signs
    base = coded[..., :PKT]
    turned = jnp.stack([-base[:, 1], base[:, 0]], 1)
    both = jnp.stack([base, turned], 1)
    gram = jnp.einsum("bqpco,bpcw->bqow", both, coded, preferred_element_type=jnp.float32)
    flat = gram.reshape(beams_here, 2, PKT * width)
    flat = jnp.pad(flat, ((0, 0), (0, 0), (0, PKT)))
    skewed = flat.reshape(beams_here, 2, PKT, width + 1)[..., 1 : LAGS + 1]
    secs = PKT // SEC_LEN
    sections = skewed.reshape(beams_here, 2, secs, SEC_LEN, LAGS).sum(3)
    gates = lax.dynamic_slice_in_dim(gate_map, (here % groups) * secs, secs)
    hot = (jnp.arange(GATES)[:, None] == gates[None, :]).astype(jnp.float32)
    scale = 1.0 / math.sqrt(tms * chunks * PKT / GATES)
    term = jnp.einsum("gs,bqsl->gbql", hot, sections * scale, precision=lax.Precision.HIGHEST)
    parts = term.reshape(tms, GATES // tms, beams_here, 2 * LAGS)
    arrived = lax.all_to_all(parts, "tm", split_axis=0, concat_axis=0, tiled=True)
    return arrived.sum(axis=0)


def solution(mesh):
    placed = (P(None, "sub", "tm"), P(None, None, "sub"), P(), P())
    return jax.shard_map(
        body, mesh=mesh, in_specs=placed, out_specs=P("tm", "sub", None), check_vma=False
    )
```

profile of v0, /device:TPU:1, one launch (start us, length us, event | category | flops | bytes accessed | tf_op | source)
XLA Modules:
  0.0 168.2 jit_solution(5255172290160874527)
XLA Ops:
  0.0 1.5 fusion.20
  1.6 0.1 pad_maximum_fusion.1
  1.7 0.2 copy.38
  1.9 0.2 reshape.169
  2.1 27.9 %fusion.19 = (bf16[1,540,4096]{2,0,1:T(2,128)(2,1)}, bf16[1,540,4096]{2,0,1:T(2,128)(2,1)}) fusion(bf16[2,540,4096]{2,0,1:T(2,128)(2,1)} %param.4), kind=kLoop, calls=%fused_computation.51 | loop fusion | bytes 17694720 | tf_op jit(solution)/shard_map/slice | solution.py:31
  30.0 0.2 copy.40
  30.2 0.2 reshape.170
  30.4 0.0 copy-start
  30.4 8.9 %fusion = f32[200,4096]{1,0:T(8,128)S(1)} fusion(bf16[200,540]{1,0:T(8,128)(2,1)S(1)} %reshape.169, bf16[1,540,4096]{2,0,1:T(2,128)(2,1)} %get-tuple-element.8), kind=kOutput, calls=%fused_computation.5 | convolution fusion | flops 884736000 | bytes 7916480 | tf_op jit(solution)/shard_map/dot_general | solution.py:30
  39.3 0.0 copy-done
  39.3 5.4 %convolution_add_fusion = f32[200,4096]{1,0:T(8,128)S(1)} fusion(f32[200,4096]{1,0:T(8,128)S(1)} %fusion, bf16[200,540]{1,0:T(8,128)(2,1)S(1)} %reshape.170, bf16[1,540,4096]{2,0,1:T(2,128)(2,1)S(1)} %copy-done), kind=kOutput, calls=%fused_computation.2 | convolution fusion | flops 885555200 | bytes 11193280 | tf_op jit(solution)/shard_map/dot_general | solution.py:30
  44.7 2.2 %reshape.171 = f32[4,50,4096]{2,1,0:T(8,128)} reshape(f32[200,4096]{1,0:T(8,128)S(1)} %convolution_add_fusion) | data formatting | bytes 6553600 | tf_op jit(solution)/shard_map/reshape | solution.py:33
  47.0 0.0 copy-start.1
  47.0 5.2 %all-to-all-start = ((f32[4,50,4096]{2,1,0:T(8,128)}), f32[4,50,4096]{2,1,0:T(8,128)}, u32[]{:S(2)}, u32[]{:S(2)}) async-start(f32[4,50,4096]{2,1,0:T(8,128)} %reshape.171), calls=%async_computation | async-start | bytes 7340032 | tf_op jit(solution)/shard_map/all_to_all | solution.py:34
  52.1 0.0 copy-done.1
  52.1 0.1 copy.45
  52.2 0.6 gather_fusion
  52.9 42.8 %all-to-all-done = f32[4,50,4096]{2,1,0:T(8,128)} async-done(((f32[4,50,4096]{2,1,0:T(8,128)}), f32[4,50,4096]{2,1,0:T(8,128)}, u32[]{:S(2)}, u32[]{:S(2)}) %all-to-all-start) | async-done | bytes 3276832 | tf_op jit(solution)/shard_map/all_to_all | solution.py:34
  95.7 2.4 %reduce_sum.27 = bf16[50,4096]{1,0:T(8,128)(2,1)S(1)} reduce(f32[4,50,4096]{2,1,0:T(8,128)} %all-to-all-done, f32[]{:T(128)} %constant.78.clone.1), dimensions={0}, to_apply=%region_0.0 | reduce | flops 614400 | bytes 3686404 | tf_op jit(solution)/shard_map/reduce_sum | solution.py:35
  98.1 0.0 copy-start.2
  98.1 1.3 convert_element_type.18
  99.4 0.7 copy.44
  100.2 5.9 %collective-permute-start.1 = (bf16[25,2,128,32]{2,3,1,0:T(8,128)(2,1)S(1)}, bf16[25,2,128,32]{2,3,1,0:T(8,128)(2,1)S(1)}, u32[]{:S(2)}, u32[]{:S(2)}) collective-permute-start(bf16[25,2,128,32]{2,3,1,0:T(8,128)(2,1)S(1)} %copy.44), channel_id=1, source_target_pairs={{2,0},{3,1},{4,2},{5,3},{6,4},{7,5},{8,6},{9,7},{10,8},{11,9},{12,... | collective-permute-start | bytes 1228808 | tf_op jit(solution)/shard_map/ppermute | solution.py:21
  106.1 1.7 collective-permute-start
  107.8 0.6 gather_fusion.1
  108.4 0.0 copy-done.2
  108.4 0.1 dynamic_slice.3
  108.5 5.0 %collective-permute-done.1 = bf16[25,2,128,32]{2,3,1,0:T(8,128)(2,1)S(1)} collective-permute-done((bf16[25,2,128,32]{2,3,1,0:T(8,128)(2,1)S(1)}, bf16[25,2,128,32]{2,3,1,0:T(8,128)(2,1)S(1)}, u32[]{:S(2)}, u32[]{:S(2)}) %collective-permute-start.1) | collective-permute-done | bytes 409632 | tf_op jit(solution)/shard_map/ppermute | solution.py:21
  113.5 0.2 slice.47
  113.6 2.2 %collective-permute-done = bf16[25,2,128,32]{2,3,1,0:T(8,128)(2,1)S(1)} collective-permute-done((bf16[25,2,128,32]{2,3,1,0:T(8,128)(2,1)S(1)}, bf16[25,2,128,32]{2,3,1,0:T(8,128)(2,1)S(1)}, u32[]{:S(2)}, u32[]{:S(2)}) %collective-permute-start) | collective-permute-done | bytes 409632 | tf_op jit(solution)/shard_map/ppermute | solution.py:21
  115.8 0.2 slice.46
  116.0 0.1 pad_select_fusion
  116.2 0.1 pad_select_fusion.1
  116.3 0.3 maximum_multiply_fusion
  116.7 0.1 slice_bitcast_fusion
  116.8 0.6 convolution_bitcast_fusion
  117.3 0.8 reshape.172
  118.2 0.2 pad.6
  118.4 1.8 %reshape.173 = f32[25,2,32,97]{3,2,1,0:T(8,128)S(1)} reshape(f32[25,2,3104]{2,1,0:T(2,128)S(1)} %pad.6) | data formatting | bytes 1241600 | tf_op jit(solution)/shard_map/reshape | solution.py:63
  120.2 0.3 slice.51
  120.5 1.0 reduce_sum.28
  121.5 2.7 %fusion.5 = f32[128,25,2,64]{0,3,2,1:T(8,128)} fusion(f32[25,2,16,64]{3,2,1,0:T(8,128)S(1)} %reduce_sum.28, s32[16]{0:T(128)S(1)} %dynamic_slice.3), kind=kOutput, calls=%fused_computation.14 | convolution fusion | flops 78696448 | bytes 1843264 | tf_op jit(solution)/shard_map/gs,bqsl->gbql/dot_general | solution.py:69
  124.2 3.9 %copy.48 = f32[128,25,2,64]{3,2,0,1:T(2,128)S(1)} copy(f32[128,25,2,64]{0,3,2,1:T(8,128)} %fusion.5) | data formatting | bytes 3276800 | tf_op jit(solution)/shard_map/gs,bqsl->gbql/dot_general | solution.py:69
  128.1 3.3 %reshape.175 = f32[32,4,25,128]{3,1,0,2:T(4,128)} reshape(f32[128,25,2,64]{3,2,0,1:T(2,128)S(1)} %copy.48) | data formatting | bytes 3276800 | tf_op jit(solution)/shard_map/reshape | solution.py:70
  131.3 1.7 %copy.49 = f32[32,4,25,128]{3,1,2,0:T(4,128)S(1)} copy(f32[32,4,25,128]{3,1,0,2:T(4,128)} %reshape.175) | data formatting | bytes 3276800 | tf_op jit(solution)/shard_map/reshape | solution.py:70
  133.1 34.3 %all_to_all.10 = f32[32,4,25,128]{3,1,2,0:T(4,128)S(1)} all-to-all(f32[32,4,25,128]{3,1,2,0:T(4,128)S(1)} %copy.49), channel_id=1, replica_groups=mesh['sub'=4,'tm'=32] {'tm'}, dimensions={0} | all-to-all | bytes 3276800 | tf_op jit(solution)/shard_map/all_to_all | solution.py:71
  167.3 0.9 reduce_sum.29
  (10 shorter events, 0.2 us)
Async XLA Ops:
  30.4 8.9 %copy-start = (bf16[1,540,4096]{2,0,1:T(2,128)(2,1)S(1)}, bf16[1,540,4096]{2,0,1:T(2,128)(2,1)}, u32[]{:S(2)}) copy-start(bf16[1,540,4096]{2,0,1:T(2,128)(2,1)} %get-tuple-element.7) | copy-start | bytes 13271044
  47.0 5.2 %copy-start.1 = (s32[32,16]{0,1:T(8,128)S(1)}, s32[32,16]{0,1:T(8,128)}, u32[]{:S(2)}) copy-start(s32[32,16]{0,1:T(8,128)} %param.6) | copy-start | bytes 6148
  47.0 48.8 %all-to-all-start = ((f32[4,50,4096]{2,1,0:T(8,128)}), f32[4,50,4096]{2,1,0:T(8,128)}, u32[]{:S(2)}, u32[]{:S(2)}) async-start(f32[4,50,4096]{2,1,0:T(8,128)} %reshape.171), calls=%async_computation | async-start | bytes 7340032 | tf_op jit(solution)/shard_map/all_to_all | solution.py:34
  98.1 10.3 %copy-start.2 = (s32[256]{0:T(256)S(1)}, s32[256]{0:T(256)}, u32[]{:S(2)}) copy-start(s32[256]{0:T(256)} %param.7) | copy-start | bytes 3076
  100.2 13.3 %collective-permute-start.1 = (bf16[25,2,128,32]{2,3,1,0:T(8,128)(2,1)S(1)}, bf16[25,2,128,32]{2,3,1,0:T(8,128)(2,1)S(1)}, u32[]{:S(2)}, u32[]{:S(2)}) collective-permute-start(bf16[25,2,128,32]{2,3,1,0:T(8,128)(2,1)S(1)} %copy.44), channel_id=1, source_target_pairs={{2,0},{3,1},{4,2},{5,3},{6,4},{7,5},{8,6},{9,7},{10,8},{11,9},{12,... | collective-permute-start | bytes 1228808 | tf_op jit(solution)/shard_map/ppermute | solution.py:21
  106.1 9.7 %collective-permute-start = (bf16[25,2,128,32]{2,3,1,0:T(8,128)(2,1)S(1)}, bf16[25,2,128,32]{2,3,1,0:T(8,128)(2,1)S(1)}, u32[]{:S(2)}, u32[]{:S(2)}) collective-permute-start(bf16[25,2,128,32]{2,3,1,0:T(8,128)(2,1)S(1)} %copy.44), channel_id=1, source_target_pairs={{1,0},{2,1},{3,2},{4,3},{5,4},{6,5},{7,6},{8,7},{9,8},{10,9},{11,1... | collective-permute-start | bytes 1228808 | tf_op jit(solution)/shard_map/ppermute | solution.py:21
where the time goes:
time: 169 us; the launch traced here: 168 us
  waiting for transfers between devices  50 us (30%)
  local copies, waits for them, and re-layouts  48.3 us (29%)
  blocking collectives  34.3 us (20%)
  matrix products  17.5 us (10%)
  starting transfers between devices  12.7 us (8%)
  other arithmetic  5.18 us (3%)
    all_to_all x1, waiting for transfers between devices, form_beams(): lax.all_to_all(parts, 'sub', split_axis=0, concat_axis=0, tiled=True)  42.8 us
    all_to_all x1, blocking collectives, body(): lax.all_to_all(parts, 'tm', split_axis=0, concat_axis=0, tiled=True)  34.3 us
    slice x1, local copies, waits for them, and re-layouts, form_beams(): streams[1]  27.9 us
    dot_general x1, matrix products, form_beams(): jnp.dot(on_real, streams[0], preferred_element_type=jnp.float32)  8.93 us
    ppermute x2, starting transfers between devices, from_next(): lax.ppermute(block, axis, [((i + distance) % count, i) for i in range(cou...  7.57 us
    ppermute x2, waiting for transfers between devices, from_next(): lax.ppermute(block, axis, [((i + distance) % count, i) for i in range(cou...  7.15 us
    dot_general x1, matrix products, form_beams(): jnp.dot(on_imag, streams[1], preferred_element_type=jnp.float32)  5.38 us
    all_to_all x1, starting transfers between devices, form_beams(): lax.all_to_all(parts, 'sub', split_axis=0, concat_axis=0, tiled=True)  5.15 us
  transfers between devices with their start and end apart: 3, of which 3 were waited for; matrix products, arithmetic and copies ran while one was open for 1% of the time, Pallas kernels for 0%

commit v1 on v0

v1 whole, which is shorter than its diff:
```python
import functools
import math

import jax
import jax.numpy as jnp
from jax import lax
from jax.experimental import pallas as pl
from jax.experimental.pallas import tpu as pltpu
from jax.sharding import PartitionSpec as P

PKT = 32
IPP_LEN = 512
LAGS = 64
NCODES = 32
NBAUD = 16
BAUD_LEN = 8
SEC_LEN = 2
GATES = 128
NSEC = 256
LANES = 128
SUBS = 4
TMS = 32
BEAMS = 25
T_DEV = 4096
GROUPS = T_DEV // LANES
ROWS = 2 * GROUPS
PAD = 112
CHUNK = 5
STEPS = BEAMS // CHUNK
PART = CHUNK * ROWS
HALF = PART // 2
BLOCK = 256
BLOCKS = T_DEV // BLOCK
WIDE = BEAMS * LANES
MESH = pl.DeviceIdType.MESH


def iota(shape, dim):
    return lax.broadcasted_iota(jnp.int32, shape, dim)


def kernel(
    streams, weights, code_signs, gate_map, out,
    held, block_rows, sums, early, first, second, beams, next1, next2, signs,
    coded, skewed, own_sec, pair_sec, row_sec, picked, gate_part, core_part,
    in_sem, a_send, a_recv, b_send, b_recv, h_send, h_recv,
    p_send, p_recv, z_send, z_recv, x_send, x_recv, c_send, c_recv,
):
    y = lax.axis_index("sub")
    d = lax.axis_index("tm")
    z = d // 8
    x = (d // 2) % 4
    core = d % 2
    half = d // 16

    def ring(step):
        return (y, lax.rem(d + step + TMS, TMS))

    def sub_to(step):
        return (lax.rem(y + step, SUBS), d)

    def z_to(step):
        return (y, lax.rem(z + step, 4) * 8 + x * 2 + core)

    def x_to(step):
        return (y, z * 8 + lax.rem(x + step, 4) * 2 + core)

    other_core = (y, d + 1 - 2 * core)

    def fetch(i):
        cols = pl.ds(pl.multiple_of(i * BLOCK, BLOCK), BLOCK)
        return pltpu.make_async_copy(
            streams.at[:, :, cols], held.at[:, :, cols], in_sem.at[i]
        )

    for i in range(BLOCKS):
        fetch(i).start()

    barrier = pltpu.get_barrier_semaphore()
    met = [sub_to(1), sub_to(3), ring(-1), ring(-2), ring(1), ring(2)]
    met += [z_to(1), z_to(2), z_to(3), x_to(1), x_to(2), x_to(3), other_core]
    for device in met:
        pl.semaphore_signal(barrier, inc=1, device_id=device, device_id_type=MESH)

    w_real = weights[0]
    w_imag = weights[1]
    block_rows[...] = jnp.zeros_like(block_rows)
    block_rows[0, 0 : w_real.shape[0], :] = w_real
    block_rows[0, PAD : PAD + w_real.shape[0], :] = w_imag
    block_rows[1, 0 : w_real.shape[0], :] = -w_imag
    block_rows[1, PAD : PAD + w_real.shape[0], :] = w_real

    def form(i, carry):
        fetch(i).wait()
        cols = pl.ds(pl.multiple_of(i * BLOCK, BLOCK), BLOCK)
        product = jnp.dot(
            block_rows[0], held[0, :, cols], preferred_element_type=jnp.float32
        ) + jnp.dot(block_rows[1], held[1, :, cols], preferred_element_type=jnp.float32)
        for h in range(BLOCK // LANES):
            for part in range(2):
                sums[pl.ds(part * GROUPS + i * (BLOCK // LANES) + h, 104, stride=ROWS), :] = product[
                    part * PAD : part * PAD + 104, h * LANES : (h + 1) * LANES
                ]
        return carry

    lax.fori_loop(0, BLOCKS, form, 0)
    pl.semaphore_wait(barrier, len(met))

    def rows_of(owner, step):
        return pl.multiple_of((owner * BEAMS + step * CHUNK) * ROWS, ROWS)

    def send_far(step, way):
        start = rows_of(lax.rem(y + 2, SUBS), step) + way * HALF
        return pltpu.make_async_remote_copy(
            src_ref=sums.at[pl.ds(start, HALF), :],
            dst_ref=early.at[step, way],
            send_sem=a_send.at[step, way],
            recv_sem=a_recv.at[step, way],
            device_id=sub_to(1 if way == 0 else 3),
            device_id_type=MESH,
        )

    def send_near(step, way):
        owner = lax.rem(y + (1 if way == 0 else 3), SUBS)
        landing = first if way == 0 else second
        return pltpu.make_async_remote_copy(
            src_ref=sums.at[pl.ds(rows_of(owner, step), PART), :],
            dst_ref=landing.at[step],
            send_sem=b_send.at[step, way],
            recv_sem=b_recv.at[step, way],
            device_id=sub_to(1 if way == 0 else 3),
            device_id_type=MESH,
        )

    def send_edge(step, way):
        landing = next1 if way == 0 else next2
        rows = pl.ds(step * PART, PART)
        return pltpu.make_async_remote_copy(
            src_ref=beams.at[rows, :],
            dst_ref=landing.at[rows, :],
            send_sem=h_send.at[step, way],
            recv_sem=h_recv.at[step, way],
            device_id=ring(-1 - way),
            device_id_type=MESH,
        )

    row = iota((256, NCODES), 0)
    code_of = lax.rem(
        2 * lax.rem(4 * lax.rem(row, GROUPS) + row // 64, 16) + half, NCODES
    )
    code_hot = (code_of == iota((256, NCODES), 1)).astype(jnp.bfloat16)
    lane16 = iota((NBAUD, LANES), 1)
    baud_hot = jnp.where(
        (lax.rem(4 * d + lane16 // BAUD_LEN, NBAUD) == iota((NBAUD, LANES), 0)) & (lane16 < 96),
        1.0,
        0.0,
    ).astype(jnp.bfloat16)
    table = (2 * code_signs[...] - 1).astype(jnp.float32).astype(jnp.bfloat16)
    by_code = jnp.dot(code_hot, table, preferred_element_type=jnp.float32).astype(jnp.bfloat16)
    signs[...] = jnp.dot(by_code, baud_hot, preferred_element_type=jnp.float32).astype(jnp.bfloat16)

    def relay(step):
        for way in range(2):
            send_far(step, way).wait_recv()
            owner = lax.rem(y + (1 if way == 0 else 3), SUBS)
            rows = pl.ds(rows_of(owner, step) + way * HALF, HALF)
            sums[rows, :] = sums[rows, :] + early[step, way]
            send_near(step, way).start()

    def settle(step):
        for way in range(2):
            send_near(step, way).wait_recv()
        total = sums[pl.ds(rows_of(y, step), PART), :] + first[step] + second[step]
        beams[pl.ds(step * PART, PART), :] = total.astype(jnp.bfloat16)
        for way in range(2):
            send_edge(step, way).start()

    lane = iota((ROWS, LANES), 1)

    def passed_end(ref, step):
        rows = pl.ds(step * PART, PART)
        turned = pltpu.roll(ref[rows, :].astype(jnp.float32), 96, 1)
        above = pltpu.roll(turned, PART - 1, 0)
        last = lax.rem(iota((PART, LANES), 0), GROUPS) == GROUPS - 1
        new = jnp.where(iota((PART, LANES), 1) < 96, turned, jnp.where(last, 0.0, above))
        ref[rows, :] = new.astype(jnp.bfloat16)

    def correlate(step):
        for way in range(2):
            send_edge(step, way).wait_recv()

        @pl.when(d >= TMS - 1)
        def _():
            passed_end(next1, step)

        @pl.when(d >= TMS - 2)
        def _():
            passed_end(next2, step)

        def one_beam(k, carry):
            beam = step * CHUNK + k
            rows = pl.ds(pl.multiple_of(beam * ROWS, ROWS), ROWS)
            here, n1, n2 = beams[rows, :], next1[rows, :], next2[rows, :]
            for c in range(4):
                mixed = jnp.where(
                    lane < 32,
                    pltpu.roll(here, (128 - 32 * c) % 128, 1) if c else here,
                    jnp.where(
                        lane < 64,
                        pltpu.roll(n1, (160 - 32 * c) % 128, 1) if c != 1 else n1,
                        pltpu.roll(n2, (192 - 32 * c) % 128, 1) if c != 2 else n2,
                    ),
                )
                mixed = mixed * signs[c * ROWS : (c + 1) * ROWS, :]
                for part in range(2):
                    coded[part * 128 + c * GROUPS : part * 128 + (c + 1) * GROUPS, :] = mixed[
                        part * GROUPS : (part + 1) * GROUPS
                    ]
            later = coded[...]
            turned = jnp.concatenate([-later[128:], later[:128]], 0)
            lane_all = iota((256, LANES), 1)
            base = jnp.where(lane_all < 32, later, pltpu.roll(turned, 32, 1))
            gram = lax.dot_general(
                base, later, (((0,), (0,)), ((), ())), preferred_element_type=jnp.float32
            )
            gram = gram[0:64]
            offset = iota((64, LANES), 0)
            for bit in (1, 2, 4, 8, 16):
                gram = jnp.where((offset & bit) > 0, pltpu.roll(gram, LANES - bit, 1), gram)
            real = pltpu.roll(gram[0:32], 127, 1)
            imag = pltpu.roll(gram[32:64], 63, 1)
            skewed[...] = jnp.where(iota((32, LANES), 1) < LAGS, real, imag)
            pairs = skewed[pl.ds(0, 16, stride=2), :] + skewed[pl.ds(1, 16, stride=2), :]
            cols = pl.ds(pl.multiple_of(beam * LANES, LANES), LANES)
            own_sec[0, :, cols] = pairs[:8]
            own_sec[1, :, cols] = pairs[8:]
            return carry

        lax.fori_loop(0, CHUNK, one_beam, 0)

    for way in range(2):
        send_far(0, way).start()
    for s in range(STEPS + 2):
        if s + 1 < STEPS:
            for way in range(2):
                send_far(s + 1, way).start()
        if s < STEPS:
            relay(s)
        if 1 <= s <= STEPS:
            settle(s - 1)
        if 2 <= s:
            correlate(s - 2)

    to_pair = pltpu.make_async_remote_copy(
        src_ref=own_sec.at[1 - half],
        dst_ref=pair_sec,
        send_sem=p_send,
        recv_sem=p_recv,
        device_id=z_to(2),
        device_id_type=MESH,
    )
    to_pair.start()
    to_pair.wait_recv()
    row_sec[z] = own_sec[half] + pair_sec[...]

    def to_z(i):
        return pltpu.make_async_remote_copy(
            src_ref=row_sec.at[z],
            dst_ref=row_sec.at[z],
            send_sem=z_send.at[i - 1],
            recv_sem=z_recv.at[i - 1],
            device_id=z_to(i),
            device_id_type=MESH,
        )

    for i in (1, 2, 3):
        to_z(i).start()
    gate_row = z * 32 + iota((32, NSEC), 0)
    named = (gate_map[...] == gate_row).astype(jnp.bfloat16)
    col = iota((NSEC, 32), 1)
    col_z = col // 8
    section = 16 * (lax.rem(col_z, 2) * 8 + x * 2 + core) + 8 * (col_z // 2) + lax.rem(col, 8)
    chosen = (iota((NSEC, 32), 0) == section).astype(jnp.bfloat16)
    gate_hot = jnp.dot(named, chosen, preferred_element_type=jnp.float32)
    for i in (1, 2, 3):
        to_z(i).wait_recv()
    scale = 1.0 / math.sqrt(TMS * T_DEV / GATES)
    gathered = row_sec[...].reshape(32, WIDE)
    picked[...] = jnp.dot(gate_hot, gathered * scale, precision=lax.Precision.HIGHEST).reshape(
        4, 8, WIDE
    )

    def to_x(i):
        return pltpu.make_async_remote_copy(
            src_ref=picked.at[lax.rem(x + i, 4)],
            dst_ref=gate_part.at[i - 1],
            send_sem=x_send.at[i - 1],
            recv_sem=x_recv.at[i - 1],
            device_id=x_to(i),
            device_id_type=MESH,
        )

    for i in (1, 2, 3):
        to_x(i).start()
    for i in (1, 2, 3):
        to_x(i).wait_recv()
    core_part[0] = picked[x] + gate_part[0] + gate_part[1] + gate_part[2]
    to_core = pltpu.make_async_remote_copy(
        src_ref=core_part.at[0],
        dst_ref=core_part.at[1],
        send_sem=c_send,
        recv_sem=c_recv,
        device_id=other_core,
        device_id_type=MESH,
    )
    to_core.start()
    to_core.wait_recv()
    out[...] = core_part[0] + core_part[1]

    for step in range(STEPS):
        for way in range(2):
            send_far(step, way).wait_send()
            send_near(step, way).wait_send()
            send_edge(step, way).wait_send()
    to_pair.wait_send()
    for i in (1, 2, 3):
        to_z(i).wait_send()
        to_x(i).wait_send()
    to_core.wait_send()


def body(streams, beam_weights, code_signs, gate_map):
    dma = pltpu.SemaphoreType.DMA
    f32, bf16 = jnp.float32, jnp.bfloat16
    vmem = pl.BlockSpec(memory_space=pltpu.VMEM)
    summed = pl.pallas_call(
        kernel,
        out_shape=jax.ShapeDtypeStruct((8, WIDE), f32),
        in_specs=[pl.BlockSpec(memory_space=pl.ANY), vmem, vmem, vmem],
        out_specs=vmem,
        scratch_shapes=[
            pltpu.VMEM(streams.shape, bf16),
            pltpu.VMEM((2, 2 * PAD, streams.shape[1]), bf16),
            pltpu.VMEM((104 * ROWS, LANES), f32),
            pltpu.VMEM((STEPS, 2, HALF, LANES), f32),
            pltpu.VMEM((STEPS, PART, LANES), f32),
            pltpu.VMEM((STEPS, PART, LANES), f32),
            pltpu.VMEM((BEAMS * ROWS, LANES), bf16),
            pltpu.VMEM((BEAMS * ROWS, LANES), bf16),
            pltpu.VMEM((BEAMS * ROWS, LANES), bf16),
            pltpu.VMEM((256, LANES), bf16),
            pltpu.VMEM((256, LANES), bf16),
            pltpu.VMEM((32, LANES), f32),
            pltpu.VMEM((2, 8, WIDE), f32),
            pltpu.VMEM((8, WIDE), f32),
            pltpu.VMEM((4, 8, WIDE), f32),
            pltpu.VMEM((4, 8, WIDE), f32),
            pltpu.VMEM((3, 8, WIDE), f32),
            pltpu.VMEM((2, 8, WIDE), f32),
            dma((BLOCKS,)),
            dma((STEPS, 2)), dma((STEPS, 2)), dma((STEPS, 2)), dma((STEPS, 2)),
            dma((STEPS, 2)), dma((STEPS, 2)),
            dma, dma, dma((3,)), dma((3,)), dma((3,)), dma((3,)), dma, dma,
        ],
        compiler_params=pltpu.CompilerParams(
            collective_id=0, has_side_effects=True, vmem_limit_bytes=48 * 2**20
        ),
    )(streams, beam_weights, code_signs, gate_map.reshape(1, NSEC))
    core = lax.axis_index("tm") % 2
    mine = lax.dynamic_slice_in_dim(summed, 4 * core, 4, 0)
    return mine.reshape(4, BEAMS, LANES)


def solution(mesh):
    placed = (P(None, "sub", "tm"), P(None, None, "sub"), P(), P())
    return jax.shard_map(
        body, mesh=mesh, in_specs=placed, out_specs=P("tm", "sub", None), check_vma=False
    )
```

time: 169 us -> 87.9 us (0.52)
  Pallas kernels: 0 us -> 73.6 us
  waiting for transfers between devices: 50 us -> 0 us
  blocking collectives: 34.3 us -> 0 us
  local copies, waits for them, and re-layouts: 48.3 us -> 14.1 us
  matrix products: 17.5 us -> 0 us
  starting transfers between devices: 12.7 us -> 0 us
  other arithmetic: 5.18 us -> 0 us
    pallas_call x0 -> x1, Pallas kernels: none -> 73.6 us  [body(): pl.pallas_call(kernel, out_shape=jax.ShapeDtypeStruct((8, WIDE), f32), in...]
    all_to_all x1 -> x0, waiting for transfers between devices: 42.8 us -> none  [form_beams(): lax.all_to_all(parts, 'sub', split_axis=0, concat_axis=0, tiled=True)]
    all_to_all x1 -> x0, blocking collectives: 34.3 us -> none  [body(): lax.all_to_all(parts, 'tm', split_axis=0, concat_axis=0, tiled=True)]
    slice x5 -> x0, local copies, waits for them, and re-layouts: 30 us -> none  [the longest x1 27.9 us: form_beams(): streams[1]]
    dot_general x4 -> x0, matrix products: 17.5 us -> none  [the longest x1 8.93 us: form_beams(): jnp.dot(on_real, streams[0], preferred_element_type=jnp.float32)]
    unnamed x7 -> x9, local copies, waits for them, and re-layouts: 0.03 us -> 13.5 us
    reshape x7 -> x1, local copies, waits for them, and re-layouts: 10.2 us -> 0.64 us  [body(): return mine.reshape(4, BEAMS, LANES)]
    ppermute x2 -> x0, starting transfers between devices: 7.57 us -> none  [from_next(): lax.ppermute(block, axis, [((i + distance) % count, i) for i in range(cou...]
  transfers between devices with their start and end apart: 3 -> 0, of which waited for: 3 -> 0; matrix products, arithmetic and copies ran while one was open for 1% -> 0% of each run, Pallas kernels for 0% -> 0%
where the time goes in v1:
time: 87.9 us; the launch traced here: 87.8 us
  Pallas kernels  73.6 us (84%)
  local copies, waits for them, and re-layouts  14.1 us (16%)
    pallas_call x1, Pallas kernels, body(): pl.pallas_call(kernel, out_shape=jax.ShapeDtypeStruct((8, WIDE), f32), in...  73.6 us
    unnamed x9, local copies, waits for them, and re-layouts  13.5 us

profile of v1, /device:TPU:1, one launch (start us, length us, event | category | flops | bytes accessed | tf_op | source)
XLA Modules:
  0.0 87.8 jit_solution(12782215369133121667)
XLA Ops:
  0.0 0.0 copy-start.1
  0.0 0.0 copy-start.2
  0.0 0.0 copy-start
  0.0 13.4 %copy.5.streams = bf16[2,540,4096]{2,1,0:T(8,128)(2,1)} copy(bf16[2,540,4096]{2,0,1:T(2,128)(2,1)} %param.4) | data formatting | bytes 17694720 | tf_op args[0]
  13.4 0.0 copy-done.1
  13.4 0.0 copy-done.2
  13.5 0.1 copy.7.code_signs
  13.5 0.0 copy-done
  13.5 73.6 %shard_map.46 = f32[8,3200]{1,0:T(8,128)S(1)} custom-call(bf16[2,540,4096]{2,1,0:T(8,128)(2,1)} %copy.5.streams, bf16[2,100,540]{2,1,0:T(8,128)(2,1)S(1)} %copy.6.weights, s32[32,16]{1,0:T(8,128)S(1)} %copy.7.code_signs, s32[1,256]{1,0:T(1,128)S(1)} %bitcast.3), custom_call_target="tpu_custom_call" | custom-call | tf_op jit(solution)/shard_map/pallas_call | solution.py:336
  87.1 0.6 dynamic-slice_bitcast_fusion
  (1 shorter events, 0.0 us)
Async XLA Ops:
  0.0 13.4 %copy-start.1 = (bf16[2,100,540]{2,0,1:T(2,128)(2,1)S(1)}, bf16[2,100,540]{2,0,1:T(2,128)(2,1)}, u32[]{:S(2)}) copy-start(bf16[2,100,540]{2,0,1:T(2,128)(2,1)} %param.5) | copy-start | bytes 648004
  0.0 13.4 %copy-start.2 = (s32[32,16]{0,1:T(8,128)S(1)}, s32[32,16]{0,1:T(8,128)}, u32[]{:S(2)}) copy-start(s32[32,16]{0,1:T(8,128)} %param.6) | copy-start | bytes 6148
  0.0 13.5 %copy-start = (s32[256]{0:T(256)S(1)}, s32[256]{0:T(256)}, u32[]{:S(2)}) copy-start(s32[256]{0:T(256)} %param.7) | copy-start | bytes 3076

commit v2 on v1

v2 whole, which is shorter than its diff:
```python
import functools
import math

import jax
import jax.numpy as jnp
from jax import lax
from jax.experimental import pallas as pl
from jax.experimental.pallas import tpu as pltpu
from jax.sharding import PartitionSpec as P

PKT = 32
IPP_LEN = 512
LAGS = 64
NCODES = 32
NBAUD = 16
BAUD_LEN = 8
SEC_LEN = 2
GATES = 128
NSEC = 256
LANES = 128
SUBS = 4
TMS = 32
BEAMS = 25
T_DEV = 4096
GROUPS = T_DEV // LANES
ROWS = 2 * GROUPS
WEIGHT_TILES = 5
CHUNK = 5
STEPS = BEAMS // CHUNK
PART = CHUNK * ROWS
HALF = PART // 2
BLOCK = 256
WIDE = BEAMS * LANES
BITS = 14.0
MESH = pl.DeviceIdType.MESH


def iota(shape, dim):
    return lax.broadcasted_iota(jnp.int32, shape, dim)


def kernel(
    streams, weights, code_signs, gate_map, out,
    held, plain, block_rows, sums, early, first, second, beams, next1, next2, signs,
    coded, skewed, row_sec, picked, gate_part, far_out, near_out,
    in_sem, a_send, a_recv, b_send, b_recv, h_send, h_recv, z_send, z_recv, g_send, g_recv,
):
    y = lax.axis_index("sub")
    d = lax.axis_index("tm")
    z = d // 8
    half = d // 16

    def ring(step):
        return (y, lax.rem(d + step + TMS, TMS))

    def sub_to(step):
        return (lax.rem(y + step, SUBS), d)

    def z_to(step):
        return (y, lax.rem(z + step, 4) * 8 + lax.rem(d, 8))

    def row_to(step):
        return (y, z * 8 + lax.rem(d + step, 8))

    def fetch(i):
        return pltpu.make_async_copy(streams.at[:, i], held.at[i], in_sem.at[i])

    for i in range(GROUPS):
        fetch(i).start()

    barrier = pltpu.get_barrier_semaphore()
    met = [sub_to(1), sub_to(3), ring(-1), ring(-2), ring(1), ring(2)]
    met += [z_to(i) for i in (1, 2, 3)] + [row_to(i) for i in range(1, 8)]
    for device in met:
        pl.semaphore_signal(barrier, inc=1, device_id=device, device_id_type=MESH)

    channels = weights.shape[2]
    stacked = weights[...].reshape(2 * weights.shape[0], channels)
    wide_rows = stacked.astype(jnp.float32)
    count = wide_rows.shape[0]
    odd = lax.rem(iota(wide_rows.shape, 0), 2) == 1
    turned_rows = jnp.where(odd, pltpu.roll(wide_rows, 1, 0), -pltpu.roll(wide_rows, count - 1, 0))
    plain[...] = jnp.zeros_like(plain)
    plain[0, :, 0:channels] = stacked
    plain[1, :, 0:channels] = turned_rows.astype(jnp.bfloat16)
    source = iota((BLOCK, BLOCK), 0)
    spread = (
        2 * lax.rem(source, LANES) + source // LANES == iota((BLOCK, BLOCK), 1)
    ).astype(jnp.bfloat16)
    for t in range(WEIGHT_TILES):
        cols = slice(t * LANES, (t + 1) * LANES)
        pair = jnp.concatenate([plain[0, :, cols], plain[1, :, cols]], 1)
        block_rows[:, t * BLOCK : (t + 1) * BLOCK] = jnp.dot(
            pair, spread, preferred_element_type=jnp.float32
        ).astype(jnp.bfloat16)
    samples = held.reshape(GROUPS, 2 * channels, LANES)

    def form(i, carry):
        for h in range(2):
            fetch(2 * i + h).wait()
        product = jnp.dot(
            block_rows[:, 0 : 2 * channels],
            jnp.concatenate([samples[2 * i], samples[2 * i + 1]], 1),
            preferred_element_type=jnp.float32,
        )
        for h in range(2):
            sums[pl.ds(2 * i + h, count, stride=GROUPS), :] = product[:, h * LANES : (h + 1) * LANES]
        top = jnp.max(jnp.abs(product).reshape(count // 8, 8, BLOCK), axis=0)
        return jnp.maximum(carry, top)

    top = lax.fori_loop(0, GROUPS // 2, form, jnp.zeros((8, BLOCK), jnp.float32))
    top = jnp.maximum(jnp.max(top, axis=(0, 1), keepdims=True), 1e-30)
    level = jnp.broadcast_to(jnp.ceil(jnp.log2(top)), (16, LANES))
    pl.semaphore_wait(barrier, len(met))

    def rows_of(owner, step):
        return pl.multiple_of((owner * BEAMS + step * CHUNK) * ROWS, ROWS)

    def packed(value, power):
        steps = value.reshape(-1, 16, LANES) * jnp.exp2(BITS - power)[None]
        return jnp.round(steps).astype(jnp.int32).astype(jnp.int16).reshape(-1, LANES)

    def unpacked(ref, count):
        power = ref[count : count + 16, :].astype(jnp.int32).astype(jnp.float32)
        steps = ref[0:count, :].astype(jnp.int32).astype(jnp.float32)
        value = steps.reshape(-1, 16, LANES) * jnp.exp2(power - BITS)[None]
        return value.reshape(count, LANES), power

    def ways(way):
        return 1 if way == 0 else 3

    def send_far(step, way):
        return pltpu.make_async_remote_copy(
            src_ref=far_out.at[step, way],
            dst_ref=early.at[step, way],
            send_sem=a_send.at[step, way],
            recv_sem=a_recv.at[step, way],
            device_id=sub_to(ways(way)),
            device_id_type=MESH,
        )

    def send_near(step, way):
        landing = first if way == 0 else second
        return pltpu.make_async_remote_copy(
            src_ref=near_out.at[step, way],
            dst_ref=landing.at[step],
            send_sem=b_send.at[step, way],
            recv_sem=b_recv.at[step, way],
            device_id=sub_to(ways(way)),
            device_id_type=MESH,
        )

    def launch(step):
        for way in range(2):
            start = rows_of(lax.rem(y + 2, SUBS), step) + way * HALF
            far_out[step, way, 0:HALF, :] = packed(sums[pl.ds(start, HALF), :], level)
            far_out[step, way, HALF : HALF + 16, :] = level.astype(jnp.int32).astype(jnp.int16)
            send_far(step, way).start()

    def send_edge(step, way):
        landing = next1 if way == 0 else next2
        rows = pl.ds(step * PART, PART)
        return pltpu.make_async_remote_copy(
            src_ref=beams.at[rows, :],
            dst_ref=landing.at[rows, :],
            send_sem=h_send.at[step, way],
            recv_sem=h_recv.at[step, way],
            device_id=ring(-1 - way),
            device_id_type=MESH,
        )

    row = iota((256, NCODES), 0)
    code_of = lax.rem(
        2 * lax.rem(4 * lax.rem(row, GROUPS) + row // 64, 16) + half, NCODES
    )
    code_hot = (code_of == iota((256, NCODES), 1)).astype(jnp.bfloat16)
    lane16 = iota((NBAUD, LANES), 1)
    baud_hot = jnp.where(
        (lax.rem(4 * d + lane16 // BAUD_LEN, NBAUD) == iota((NBAUD, LANES), 0)) & (lane16 < 96),
        1.0,
        0.0,
    ).astype(jnp.bfloat16)
    table = (2 * code_signs[...] - 1).astype(jnp.float32).astype(jnp.bfloat16)
    by_code = jnp.dot(code_hot, table, preferred_element_type=jnp.float32).astype(jnp.bfloat16)
    signs[...] = jnp.dot(by_code, baud_hot, preferred_element_type=jnp.float32).astype(jnp.bfloat16)

    def relay(step):
        for way in range(2):
            send_far(step, way).wait_recv()
            start = rows_of(lax.rem(y + ways(way), SUBS), step)
            passed, power = unpacked(early.at[step, way], HALF)
            both = jnp.maximum(power, level) + 1
            mine = slice(way * HALF, (way + 1) * HALF)
            rest = slice((1 - way) * HALF, (2 - way) * HALF)
            near_out[step, way, mine, :] = packed(
                sums[pl.ds(start + way * HALF, HALF), :] + passed, both
            )
            near_out[step, way, rest, :] = packed(
                sums[pl.ds(start + (1 - way) * HALF, HALF), :], both
            )
            near_out[step, way, PART : PART + 16, :] = both.astype(jnp.int32).astype(jnp.int16)
            send_near(step, way).start()

    def settle(step):
        for way in range(2):
            send_near(step, way).wait_recv()
        total = sums[pl.ds(rows_of(y, step), PART), :]
        total += unpacked(first.at[step], PART)[0] + unpacked(second.at[step], PART)[0]
        beams[pl.ds(step * PART, PART), :] = total.astype(jnp.bfloat16)
        for way in range(2):
            send_edge(step, way).start()

    lane = iota((ROWS, LANES), 1)

    def passed_end(ref, step):
        rows = pl.ds(step * PART, PART)
        turned = pltpu.roll(ref[rows, :].astype(jnp.float32), 96, 1)
        above = pltpu.roll(turned, PART - 1, 0)
        last = lax.rem(iota((PART, LANES), 0), GROUPS) == GROUPS - 1
        new = jnp.where(iota((PART, LANES), 1) < 96, turned, jnp.where(last, 0.0, above))
        ref[rows, :] = new.astype(jnp.bfloat16)

    def correlate(step):
        for way in range(2):
            send_edge(step, way).wait_recv()

        @pl.when(d >= TMS - 1)
        def _():
            passed_end(next1, step)

        @pl.when(d >= TMS - 2)
        def _():
            passed_end(next2, step)

        def one_beam(k, carry):
            beam = step * CHUNK + k
            rows = pl.ds(pl.multiple_of(beam * ROWS, ROWS), ROWS)
            here, n1, n2 = beams[rows, :], next1[rows, :], next2[rows, :]
            for c in range(4):
                mixed = jnp.where(
                    lane < 32,
                    pltpu.roll(here, (128 - 32 * c) % 128, 1) if c else here,
                    jnp.where(
                        lane < 64,
                        pltpu.roll(n1, (160 - 32 * c) % 128, 1) if c != 1 else n1,
                        pltpu.roll(n2, (192 - 32 * c) % 128, 1) if c != 2 else n2,
                    ),
                )
                mixed = mixed * signs[c * ROWS : (c + 1) * ROWS, :]
                for part in range(2):
                    coded[part * 128 + c * GROUPS : part * 128 + (c + 1) * GROUPS, :] = mixed[
                        part * GROUPS : (part + 1) * GROUPS
                    ]
            later = coded[...]
            turned = jnp.concatenate([-later[128:], later[:128]], 0)
            lane_all = iota((256, LANES), 1)
            base = jnp.where(lane_all < 32, later, pltpu.roll(turned, 32, 1))
            gram = lax.dot_general(
                base, later, (((0,), (0,)), ((), ())), preferred_element_type=jnp.float32
            )
            gram = gram[0:64]
            offset = iota((64, LANES), 0)
            for bit in (1, 2, 4, 8, 16):
                gram = jnp.where((offset & bit) > 0, pltpu.roll(gram, LANES - bit, 1), gram)
            real = pltpu.roll(gram[0:32], 127, 1)
            imag = pltpu.roll(gram[32:64], 63, 1)
            skewed[...] = jnp.where(iota((32, LANES), 1) < LAGS, real, imag)
            pairs = skewed[pl.ds(0, 16, stride=2), :] + skewed[pl.ds(1, 16, stride=2), :]
            cols = pl.ds(pl.multiple_of(k * LANES, LANES), LANES)
            row_sec[step, z, :, cols] = pairs
            return carry

        lax.fori_loop(0, CHUNK, one_beam, 0)

    def send_z(step, i):
        return pltpu.make_async_remote_copy(
            src_ref=row_sec.at[step, z],
            dst_ref=row_sec.at[step, z],
            send_sem=z_send.at[step, i - 1],
            recv_sem=z_recv.at[step, i - 1],
            device_id=z_to(i),
            device_id_type=MESH,
        )

    def send_gates(step, i):
        return pltpu.make_async_remote_copy(
            src_ref=picked.at[step, lax.rem(d + i, 8)],
            dst_ref=gate_part.at[step, i - 1],
            send_sem=g_send.at[step, i - 1],
            recv_sem=g_recv.at[step, i - 1],
            device_id=row_to(i),
            device_id_type=MESH,
        )

    gate_row = z * 32 + iota((32, NSEC), 0)
    named = (gate_map[...] == gate_row).astype(jnp.bfloat16)
    col = iota((NSEC, 64), 1)
    section = 16 * (lax.rem(col // 16, 2) * 8 + lax.rem(d, 8)) + lax.rem(col, 16)
    chosen = (iota((NSEC, 64), 0) == section).astype(jnp.bfloat16)
    scale = 1.0 / math.sqrt(TMS * T_DEV / GATES)
    gate_hot = jnp.dot(named, chosen, preferred_element_type=jnp.float32)

    def route(step):
        for i in (1, 2, 3):
            send_z(step, i).wait_recv()
        gathered = row_sec[step].reshape(64, CHUNK * LANES) * scale
        gates = jnp.dot(gate_hot, gathered, precision=lax.Precision.HIGHEST)
        for k in range(8):
            picked[step, k] = gates[4 * k : 4 * k + 4]
        for i in range(1, 8):
            send_gates(step, i).start()

    def finish(step):
        total = picked[step, lax.rem(d, 8)]
        for i in range(1, 8):
            send_gates(step, i).wait_recv()
            total += gate_part[step, i - 1]
        out[:, step * CHUNK * LANES : (step + 1) * CHUNK * LANES] = total

    launch(0)
    for s in range(STEPS + 4):
        if s + 1 < STEPS:
            launch(s + 1)
        if s < STEPS:
            relay(s)
        if 1 <= s <= STEPS:
            settle(s - 1)
        if 2 <= s <= STEPS + 1:
            correlate(s - 2)
            for i in (1, 2, 3):
                send_z(s - 2, i).start()
        if 3 <= s <= STEPS + 2:
            route(s - 3)
        if 4 <= s:
            finish(s - 4)

    for step in range(STEPS):
        for way in range(2):
            send_far(step, way).wait_send()
            send_near(step, way).wait_send()
            send_edge(step, way).wait_send()
        for i in (1, 2, 3):
            send_z(step, i).wait_send()
        for i in range(1, 8):
            send_gates(step, i).wait_send()


def body(streams, beam_weights, code_signs, gate_map):
    dma = pltpu.SemaphoreType.DMA
    channels = streams.shape[1]
    tiles = streams.reshape(2, channels, GROUPS, LANES).transpose(1, 2, 0, 3)
    paired = beam_weights.transpose(1, 0, 2)
    f32, bf16, i16 = jnp.float32, jnp.bfloat16, jnp.int16
    vmem = pl.BlockSpec(memory_space=pltpu.VMEM)
    summed = pl.pallas_call(
        kernel,
        out_shape=jax.ShapeDtypeStruct((4, WIDE), f32),
        in_specs=[pl.BlockSpec(memory_space=pl.ANY), vmem, vmem, vmem],
        out_specs=vmem,
        scratch_shapes=[
            pltpu.VMEM((GROUPS, channels, 2, LANES), bf16),
            pltpu.VMEM((2, 200, WEIGHT_TILES * LANES), bf16),
            pltpu.VMEM((200, WEIGHT_TILES * BLOCK), bf16),
            pltpu.VMEM((100 * ROWS, LANES), f32),
            pltpu.VMEM((STEPS, 2, HALF + 16, LANES), i16),
            pltpu.VMEM((STEPS, PART + 16, LANES), i16),
            pltpu.VMEM((STEPS, PART + 16, LANES), i16),
            pltpu.VMEM((BEAMS * ROWS, LANES), bf16),
            pltpu.VMEM((BEAMS * ROWS, LANES), bf16),
            pltpu.VMEM((BEAMS * ROWS, LANES), bf16),
            pltpu.VMEM((256, LANES), bf16),
            pltpu.VMEM((256, LANES), bf16),
            pltpu.VMEM((32, LANES), f32),
            pltpu.VMEM((STEPS, 4, 16, CHUNK * LANES), f32),
            pltpu.VMEM((STEPS, 8, 4, CHUNK * LANES), f32),
            pltpu.VMEM((STEPS, 7, 4, CHUNK * LANES), f32),
            pltpu.VMEM((STEPS, 2, HALF + 16, LANES), i16),
            pltpu.VMEM((STEPS, 2, PART + 16, LANES), i16),
            dma((GROUPS,)),
            dma((STEPS, 2)), dma((STEPS, 2)), dma((STEPS, 2)), dma((STEPS, 2)),
            dma((STEPS, 2)), dma((STEPS, 2)),
            dma((STEPS, 3)), dma((STEPS, 3)), dma((STEPS, 7)), dma((STEPS, 7)),
        ],
        compiler_params=pltpu.CompilerParams(
            collective_id=0, has_side_effects=True, vmem_limit_bytes=48 * 2**20
        ),
    )(tiles, paired, code_signs, gate_map.reshape(1, NSEC))
    return summed.reshape(4, BEAMS, LANES)


def solution(mesh):
    placed = (P(None, "sub", "tm"), P(None, None, "sub"), P(), P())
    return jax.shard_map(
        body, mesh=mesh, in_specs=placed, out_specs=P("tm", "sub", None), check_vma=False
    )
```

time: 87.9 us -> 66.1 us (0.75)
  local copies, waits for them, and re-layouts: 14.1 us -> 3.02 us
  Pallas kernels: 73.6 us -> 62.9 us
    pallas_call x1, Pallas kernels: 73.6 us -> 62.9 us  [body(): pl.pallas_call(kernel, out_shape=jax.ShapeDtypeStruct((4, WIDE), f32), in...]
    unnamed x9 -> x6, local copies, waits for them, and re-layouts: 13.5 us -> 3.02 us
where the time goes in v2:
time: 66.1 us; the launch traced here: 65.9 us
  Pallas kernels  62.9 us (95%)
  local copies, waits for them, and re-layouts  3.02 us (5%)
    pallas_call x1, Pallas kernels, body(): pl.pallas_call(kernel, out_shape=jax.ShapeDtypeStruct((4, WIDE), f32), in...  62.9 us
    unnamed x6, local copies, waits for them, and re-layouts  3.02 us

profile of v2, /device:TPU:1, one launch (start us, length us, event | category | flops | bytes accessed | tf_op | source)
XLA Modules:
  0.0 65.9 jit_solution(2327378116949057228)
XLA Ops:
  0.0 0.8 %copy.7.code_signs = s32[32,16]{1,0:T(8,128)S(1)} copy(s32[32,16]{0,1:T(8,128)} %param.6) | data formatting | bytes 4096 | tf_op args[2]
  0.8 0.0 copy-start
  0.8 0.9 %copy-done = bf16[2,100,540]{2,0,1:T(2,128)(2,1)S(1)} copy-done((bf16[2,100,540]{2,0,1:T(2,128)(2,1)S(1)}, bf16[2,100,540]{2,0,1:T(2,128)(2,1)}, u32[]{:S(2)}) %copy-start) | copy-done | bytes 216024
  1.7 0.0 copy-start.1
  1.7 0.7 %copy-done.1 = s32[256]{0:T(256)S(1)} copy-done((s32[256]{0:T(256)S(1)}, s32[256]{0:T(256)}, u32[]{:S(2)}) %copy-start.1) | copy-done | bytes 1048
  2.4 62.9 %shard_map.46 = f32[4,3200]{1,0:T(4,128)S(1)} custom-call(bf16[540,32,2,128]{3,2,1,0:T(2,128)(2,1)} %bitcast.9, bf16[100,2,540]{2,1,0:T(2,128)(2,1)S(1)} %bitcast.6, s32[32,16]{1,0:T(8,128)S(1)} %copy.7.code_signs, s32[1,256]{1,0:T(1,128)S(1)} %bitcast.8), custom_call_target="tpu_custom_call" | custom-call | tf_op jit(solution)/shard_map/pallas_call | solution.py:355
  65.3 0.6 copy.10
Async XLA Ops:
  0.8 0.9 %copy-start = (bf16[2,100,540]{2,0,1:T(2,128)(2,1)S(1)}, bf16[2,100,540]{2,0,1:T(2,128)(2,1)}, u32[]{:S(2)}) copy-start(bf16[2,100,540]{2,0,1:T(2,128)(2,1)} %param.5) | copy-start | bytes 648004
  1.7 0.7 %copy-start.1 = (s32[256]{0:T(256)S(1)}, s32[256]{0:T(256)}, u32[]{:S(2)}) copy-start(s32[256]{0:T(256)} %param.7) | copy-start | bytes 3076

commit v3 on v2

v3 whole, which is shorter than its diff:
```python
import functools
import math

import jax
import jax.numpy as jnp
from jax import lax
from jax.experimental import pallas as pl
from jax.experimental.pallas import tpu as pltpu
from jax.sharding import PartitionSpec as P

PKT = 32
IPP_LEN = 512
LAGS = 64
NCODES = 32
NBAUD = 16
BAUD_LEN = 8
SEC_LEN = 2
GATES = 128
NSEC = 256
LANES = 128
SUBS = 4
TMS = 32
BEAMS = 25
T_DEV = 4096
GROUPS = T_DEV // LANES
ROWS = 2 * GROUPS
PACKED = 16
SPAN = 4
WEIGHT_TILES = 5
CHUNK = 5
STEPS = BEAMS // CHUNK
LINES = 2 * CHUNK
PART = LINES * PACKED
HALF = PART // 2
BLOCK = 256
WIDE = BEAMS * LANES
BITS = 14.9
EARLY_RELAYS = ((), (0, 1), (2, 3), (4,))
EARLY_SETTLES = ((), (), (0,), (1, 2))
LATE_SETTLES = ((3,), (4,))
MESH = pl.DeviceIdType.MESH


def iota(shape, dim):
    return lax.broadcasted_iota(jnp.int32, shape, dim)


def kernel(
    streams, weights, code_signs, gate_map, out,
    held, plain, block_rows, sums, early, first, second, beams, signs,
    coded, skewed, row_sec, picked, gate_part, far_out, near_out,
    in_sem, a_send, a_recv, b_send, b_recv, h_send, h_recv, z_send, z_recv, g_send, g_recv,
):
    y = lax.axis_index("sub")
    d = lax.axis_index("tm")
    z = d // 8
    core = lax.rem(d, 2)
    based = lax.rem(d + TMS - 2 * core, TMS)

    def ring(step):
        return (y, lax.rem(d + step + TMS, TMS))

    def sub_to(step):
        return (lax.rem(y + step, SUBS), d)

    def z_to(step):
        return (y, lax.rem(z + step, 4) * 8 + lax.rem(d, 8))

    def row_to(step):
        return (y, z * 8 + lax.rem(d + step, 8))

    def fetch(i):
        return pltpu.make_async_copy(streams.at[:, i], held.at[i], in_sem.at[i])

    for i in range(GROUPS):
        fetch(i).start()

    barrier = pltpu.get_barrier_semaphore()
    met = [sub_to(1), sub_to(3), ring(-2), ring(2)]
    met += [z_to(i) for i in (1, 2, 3)] + [row_to(i) for i in range(1, 8)]
    for device in met:
        pl.semaphore_signal(barrier, inc=1, device_id=device, device_id_type=MESH)

    channels = weights.shape[2]
    stacked = weights[...].reshape(2 * weights.shape[0], channels)
    wide_rows = stacked.astype(jnp.float32)
    count = wide_rows.shape[0]
    odd = lax.rem(iota(wide_rows.shape, 0), 2) == 1
    turned_rows = jnp.where(odd, pltpu.roll(wide_rows, 1, 0), -pltpu.roll(wide_rows, count - 1, 0))
    plain[...] = jnp.zeros_like(plain)
    plain[0, :, 0:channels] = stacked
    plain[1, :, 0:channels] = turned_rows.astype(jnp.bfloat16)
    source = iota((BLOCK, BLOCK), 0)
    spread = (
        2 * lax.rem(source, LANES) + source // LANES == iota((BLOCK, BLOCK), 1)
    ).astype(jnp.bfloat16)
    for t in range(WEIGHT_TILES):
        cols = slice(t * LANES, (t + 1) * LANES)
        pair = jnp.concatenate([plain[0, :, cols], plain[1, :, cols]], 1)
        block_rows[:, t * BLOCK : (t + 1) * BLOCK] = jnp.dot(
            pair, spread, preferred_element_type=jnp.float32
        ).astype(jnp.bfloat16)
    samples = held.reshape(GROUPS, 2 * channels, LANES)

    def form(i, carry):
        for h in range(SPAN):
            fetch(SPAN * i + h).wait()
        product = jnp.dot(
            block_rows[:, 0 : 2 * channels],
            jnp.concatenate([samples[SPAN * i + h] for h in range(SPAN)], 1),
            preferred_element_type=jnp.float32,
        )
        for h in range(SPAN):
            place = SPAN * i + h
            sums[
                place // PACKED, pl.ds(lax.rem(place, PACKED), count, stride=PACKED), :
            ] = product[:, h * LANES : (h + 1) * LANES]
        top = jnp.max(jnp.abs(product).reshape(count // 8, 8, SPAN * LANES), axis=0)
        return jnp.maximum(carry, top)

    nothing = jnp.zeros((8, SPAN * LANES), jnp.float32)
    blocks = GROUPS // SPAN

    def level_of(top):
        most = jnp.maximum(jnp.max(top, axis=(0, 1), keepdims=True), 1e-30)
        return jnp.broadcast_to(jnp.ceil(jnp.log2(most)), (PACKED, LANES))

    def rows_of(owner, step):
        return pl.multiple_of((owner * BEAMS + step * CHUNK) * 2 * PACKED, PACKED)

    def packed(value, power):
        steps = value.reshape(-1, 16, LANES) * jnp.exp2(BITS - power)[None]
        return jnp.round(steps).astype(jnp.int32).astype(jnp.int16).reshape(-1, LANES)

    def unpacked(ref, count):
        power = ref[count : count + 16, :].astype(jnp.int32).astype(jnp.float32)
        steps = ref[0:count, :].astype(jnp.int32).astype(jnp.float32)
        value = steps.reshape(-1, 16, LANES) * jnp.exp2(power - BITS)[None]
        return value.reshape(count, LANES), power

    def ways(way):
        return 1 if way == 0 else 3

    def send_far(t, step, way):
        return pltpu.make_async_remote_copy(
            src_ref=far_out.at[t, step, way],
            dst_ref=early.at[t, step, way],
            send_sem=a_send.at[t, step, way],
            recv_sem=a_recv.at[t, step, way],
            device_id=sub_to(ways(way)),
            device_id_type=MESH,
        )

    def send_near(t, step, way):
        landing = first if way == 0 else second
        return pltpu.make_async_remote_copy(
            src_ref=near_out.at[t, step, way],
            dst_ref=landing.at[t, step],
            send_sem=b_send.at[t, step, way],
            recv_sem=b_recv.at[t, step, way],
            device_id=sub_to(ways(way)),
            device_id_type=MESH,
        )

    def launch(t, step):
        for way in range(2):
            start = rows_of(lax.rem(y + 2, SUBS), step) + way * HALF
            far_out[t, step, way, 0:HALF, :] = packed(sums[t, pl.ds(start, HALF), :], level[t])
            far_out[t, step, way, HALF : HALF + 16, :] = (
                level[t].astype(jnp.int32).astype(jnp.int16)
            )
            send_far(t, step, way).start()

    def send_edge(step, way):
        lines = pl.ds(step * LINES, LINES)
        return pltpu.make_async_remote_copy(
            src_ref=beams.at[2 * core, lines],
            dst_ref=beams.at[1 if way == 0 else 2 - 2 * core, lines],
            send_sem=h_send.at[step, way],
            recv_sem=h_recv.at[step, way],
            device_id=(y, d + 1 - 2 * core) if way == 0 else ring(4 * core - 2),
            device_id_type=MESH,
        )

    row = iota((256, NCODES), 0)
    code_of = lax.rem(
        2 * lax.rem(4 * lax.rem(row, GROUPS) + row // 64, 16) + based // 16, NCODES
    )
    code_hot = (code_of == iota((256, NCODES), 1)).astype(jnp.bfloat16)
    lane16 = iota((NBAUD, LANES), 1)
    baud_hot = jnp.where(
        (lax.rem(4 * based + lane16 // BAUD_LEN, NBAUD) == iota((NBAUD, LANES), 0)) & (lane16 < 96),
        1.0,
        0.0,
    ).astype(jnp.bfloat16)
    table = (2 * code_signs[...] - 1).astype(jnp.float32).astype(jnp.bfloat16)
    by_code = jnp.dot(code_hot, table, preferred_element_type=jnp.float32).astype(jnp.bfloat16)
    signs[...] = jnp.dot(by_code, baud_hot, preferred_element_type=jnp.float32).astype(jnp.bfloat16)

    def relay(t, step):
        for way in range(2):
            send_far(t, step, way).wait_recv()
            start = rows_of(lax.rem(y + ways(way), SUBS), step)
            passed, power = unpacked(early.at[t, step, way], HALF)
            both = jnp.maximum(power, level[t]) + 1
            mine = slice(way * HALF, (way + 1) * HALF)
            rest = slice((1 - way) * HALF, (2 - way) * HALF)
            near_out[t, step, way, mine, :] = packed(
                sums[t, pl.ds(start + way * HALF, HALF), :] + passed, both
            )
            near_out[t, step, way, rest, :] = packed(
                sums[t, pl.ds(start + (1 - way) * HALF, HALF), :], both
            )
            near_out[t, step, way, PART : PART + 16, :] = both.astype(jnp.int32).astype(jnp.int16)
            send_near(t, step, way).start()

    def settle(t, step):
        for way in range(2):
            send_near(t, step, way).wait_recv()
        total = sums[t, pl.ds(rows_of(y, step), PART), :]
        total += unpacked(first.at[t, step], PART)[0] + unpacked(second.at[t, step], PART)[0]
        beams[2 * core, step * LINES : (step + 1) * LINES, t] = total.astype(jnp.bfloat16).reshape(
            LINES, PACKED, LANES
        )

    def share(step):
        for way in range(2):
            send_edge(step, way).start()

    span = CHUNK * ROWS
    lane = iota((span, LANES), 1)
    offset = iota((span, LANES), 0)

    def passed_end(slot, step):
        lines = slice(step * LINES, (step + 1) * LINES)
        turned = pltpu.roll(beams[slot, lines].reshape(span, LANES).astype(jnp.float32), 96, 1)
        above = pltpu.roll(turned, span - 1, 0)
        last = lax.rem(offset, GROUPS) == GROUPS - 1
        new = jnp.where(lane < 96, turned, jnp.where(last, 0.0, above))
        beams[slot, lines] = new.astype(jnp.bfloat16).reshape(LINES, 2, PACKED, LANES)

    def correlate(step):
        for way in range(2):
            send_edge(step, way).wait()

        @pl.when(d == 1)
        def _():
            passed_end(1, step)

        @pl.when((d == 1) | (d == TMS - 2))
        def _():
            passed_end(2, step)

        lines = slice(step * LINES, (step + 1) * LINES)
        three = [beams[slot, lines].reshape(span, LANES) for slot in range(3)]
        for c in range(4):
            here, n1, n2 = [
                pltpu.roll(v, shift, 1) if shift else v
                for v, shift in ((v, (128 + 32 * (j - c)) % 128) for j, v in enumerate(three))
            ]
            mixed = jnp.where(lane < 32, here, jnp.where(lane < 64, n1, n2))
            mixed = mixed.reshape(CHUNK, ROWS, LANES) * signs[c * ROWS : (c + 1) * ROWS, :][None]
            coded[:, :, c] = mixed.reshape(CHUNK, 2, GROUPS, LANES)
        grams = []
        low = iota((256, LANES), 1) < 32
        for k in range(CHUNK):
            later = coded[k].reshape(256, LANES)
            turned = jnp.concatenate([-later[128:], later[:128]], 0)
            base = jnp.where(low, later, pltpu.roll(turned, 32, 1))
            gram = lax.dot_general(
                base, later, (((0,), (0,)), ((), ())), preferred_element_type=jnp.float32
            )
            real = jnp.concatenate(
                [pltpu.roll(gram[r : r + 8], 127 - r, 1) for r in (0, 8, 16, 24)], 0
            )
            imag = jnp.concatenate(
                [pltpu.roll(gram[r + 32 : r + 40], (191 - r) % 128, 1) for r in (0, 8, 16, 24)], 0
            )
            grams += [real, imag]
        gram = jnp.concatenate(grams, 0)
        for bit in (1, 2, 4):
            gram = jnp.where((offset & bit) > 0, pltpu.roll(gram, LANES - bit, 1), gram)
        gram = gram.reshape(CHUNK, 2, 32, LANES)
        skewed[...] = jnp.where(iota((CHUNK, 32, LANES), 2) < LAGS, gram[:, 0], gram[:, 1]).reshape(
            CHUNK * 32, LANES
        )
        pairs = skewed[pl.ds(0, CHUNK * 16, stride=2), :] + skewed[pl.ds(1, CHUNK * 16, stride=2), :]
        for k in range(CHUNK):
            row_sec[step, z, :, k * LANES : (k + 1) * LANES] = pairs[16 * k : 16 * k + 16]

    def send_z(step, i):
        return pltpu.make_async_remote_copy(
            src_ref=row_sec.at[step, z],
            dst_ref=row_sec.at[step, z],
            send_sem=z_send.at[step, i - 1],
            recv_sem=z_recv.at[step, i - 1],
            device_id=z_to(i),
            device_id_type=MESH,
        )

    def send_gates(step, i):
        return pltpu.make_async_remote_copy(
            src_ref=picked.at[step, lax.rem(d + i, 8)],
            dst_ref=gate_part.at[step, i - 1],
            send_sem=g_send.at[step, i - 1],
            recv_sem=g_recv.at[step, i - 1],
            device_id=row_to(i),
            device_id_type=MESH,
        )

    gate_row = z * 32 + iota((32, NSEC), 0)
    named = (gate_map[...] == gate_row).astype(jnp.bfloat16)
    col = iota((NSEC, 64), 1)
    origin = lax.rem(col // 16 * 8 + lax.rem(d, 8) + TMS - 2 * core, 16)
    section = 16 * origin + lax.rem(col, 16)
    chosen = (iota((NSEC, 64), 0) == section).astype(jnp.bfloat16)
    scale = 1.0 / math.sqrt(TMS * T_DEV / GATES)
    gate_hot = jnp.dot(named, chosen, preferred_element_type=jnp.float32)

    def route(step):
        for i in (1, 2, 3):
            send_z(step, i).wait_recv()
        gathered = row_sec[step].reshape(64, CHUNK * LANES) * scale
        gates = jnp.dot(gate_hot, gathered, precision=lax.Precision.HIGHEST)
        for k in range(8):
            picked[step, k] = gates[4 * k : 4 * k + 4]
        for i in range(1, 8):
            send_gates(step, i).start()

    def finish(step):
        total = picked[step, lax.rem(d, 8)]
        for i in range(1, 8):
            send_gates(step, i).wait_recv()
            total += gate_part[step, i - 1]
        out[:, step * CHUNK * LANES : (step + 1) * CHUNK * LANES] = total

    level = [None, None]
    level[0] = level_of(lax.fori_loop(0, blocks // 2, form, nothing))
    pl.semaphore_wait(barrier, len(met))
    for j in range(STEPS):
        launch(0, j)
    top = nothing
    for i in range(blocks // 2):
        top = form(blocks // 2 + i, top)
        for j in EARLY_RELAYS[i]:
            relay(0, j)
        for j in EARLY_SETTLES[i]:
            settle(0, j)
    level[1] = level_of(top)
    launch(1, 0)
    for s in range(STEPS + 4):
        if s + 1 < STEPS:
            launch(1, s + 1)
        if s < STEPS:
            relay(1, s)
        for j in LATE_SETTLES[s] if s < len(LATE_SETTLES) else ():
            settle(0, j)
        if 1 <= s <= STEPS:
            settle(1, s - 1)
            share(s - 1)
        if 2 <= s <= STEPS + 1:
            correlate(s - 2)
            for i in (1, 2, 3):
                send_z(s - 2, i).start()
        if 3 <= s <= STEPS + 2:
            route(s - 3)
        if 4 <= s:
            finish(s - 4)

    for step in range(STEPS):
        for t in range(2):
            for way in range(2):
                send_far(t, step, way).wait_send()
                send_near(t, step, way).wait_send()
        for i in (1, 2, 3):
            send_z(step, i).wait_send()
        for i in range(1, 8):
            send_gates(step, i).wait_send()


def body(streams, beam_weights, code_signs, gate_map):
    dma = pltpu.SemaphoreType.DMA
    channels = streams.shape[1]
    tiles = streams.reshape(2, channels, GROUPS, LANES).transpose(1, 2, 0, 3)
    paired = beam_weights.transpose(1, 0, 2)
    f32, bf16, i16 = jnp.float32, jnp.bfloat16, jnp.int16
    vmem = pl.BlockSpec(memory_space=pltpu.VMEM)
    summed = pl.pallas_call(
        kernel,
        out_shape=jax.ShapeDtypeStruct((4, WIDE), f32),
        in_specs=[pl.BlockSpec(memory_space=pl.ANY), vmem, vmem, vmem],
        out_specs=vmem,
        scratch_shapes=[
            pltpu.VMEM((GROUPS, channels, 2, LANES), bf16),
            pltpu.VMEM((2, 200, WEIGHT_TILES * LANES), bf16),
            pltpu.VMEM((200, WEIGHT_TILES * BLOCK), bf16),
            pltpu.VMEM((2, 200 * PACKED, LANES), f32),
            pltpu.VMEM((2, STEPS, 2, HALF + 16, LANES), i16),
            pltpu.VMEM((2, STEPS, PART + 16, LANES), i16),
            pltpu.VMEM((2, STEPS, PART + 16, LANES), i16),
            pltpu.VMEM((3, 2 * BEAMS, 2, PACKED, LANES), bf16),
            pltpu.VMEM((256, LANES), bf16),
            pltpu.VMEM((CHUNK, 2, 4, GROUPS, LANES), bf16),
            pltpu.VMEM((CHUNK * 32, LANES), f32),
            pltpu.VMEM((STEPS, 4, 16, CHUNK * LANES), f32),
            pltpu.VMEM((STEPS, 8, 4, CHUNK * LANES), f32),
            pltpu.VMEM((STEPS, 7, 4, CHUNK * LANES), f32),
            pltpu.VMEM((2, STEPS, 2, HALF + 16, LANES), i16),
            pltpu.VMEM((2, STEPS, 2, PART + 16, LANES), i16),
            dma((GROUPS,)),
            dma((2, STEPS, 2)), dma((2, STEPS, 2)), dma((2, STEPS, 2)), dma((2, STEPS, 2)),
            dma((STEPS, 2)), dma((STEPS, 2)),
            dma((STEPS, 3)), dma((STEPS, 3)), dma((STEPS, 7)), dma((STEPS, 7)),
        ],
        compiler_params=pltpu.CompilerParams(
            collective_id=0, has_side_effects=True, vmem_limit_bytes=48 * 2**20
        ),
    )(tiles, paired, code_signs, gate_map.reshape(1, NSEC))
    return summed.reshape(4, BEAMS, LANES)


def solution(mesh):
    placed = (P(None, "sub", "tm"), P(None, None, "sub"), P(), P())
    return jax.shard_map(
        body, mesh=mesh, in_specs=placed, out_specs=P("tm", "sub", None), check_vma=False
    )
```

time: 66.1 us -> 58.6 us (0.89)
  Pallas kernels: 62.9 us -> 55.3 us
    pallas_call x1, Pallas kernels: 62.9 us -> 55.3 us  [body(): pl.pallas_call(kernel, out_shape=jax.ShapeDtypeStruct((4, WIDE), f32), in...]
where the time goes in v3:
time: 58.6 us; the launch traced here: 58.4 us
  Pallas kernels  55.3 us (94%)
  local copies, waits for them, and re-layouts  3.02 us (5%)
    pallas_call x1, Pallas kernels, body(): pl.pallas_call(kernel, out_shape=jax.ShapeDtypeStruct((4, WIDE), f32), in...  55.3 us
    unnamed x6, local copies, waits for them, and re-layouts  3.02 us

profile of v3, /device:TPU:1, one launch (start us, length us, event | category | flops | bytes accessed | tf_op | source)
XLA Modules:
  0.0 58.4 jit_solution(1876496640504792568)
XLA Ops:
  0.0 0.8 %copy.7.code_signs = s32[32,16]{1,0:T(8,128)S(1)} copy(s32[32,16]{0,1:T(8,128)} %param.6) | data formatting | bytes 4096 | tf_op args[2]
  0.8 0.0 copy-start
  0.8 0.9 %copy-done = bf16[2,100,540]{2,0,1:T(2,128)(2,1)S(1)} copy-done((bf16[2,100,540]{2,0,1:T(2,128)(2,1)S(1)}, bf16[2,100,540]{2,0,1:T(2,128)(2,1)}, u32[]{:S(2)}) %copy-start) | copy-done | bytes 216024
  1.7 0.0 copy-start.1
  1.7 0.7 %copy-done.1 = s32[256]{0:T(256)S(1)} copy-done((s32[256]{0:T(256)S(1)}, s32[256]{0:T(256)}, u32[]{:S(2)}) %copy-start.1) | copy-done | bytes 1048
  2.4 55.3 %shard_map.46 = f32[4,3200]{1,0:T(4,128)S(1)} custom-call(bf16[540,32,2,128]{3,2,1,0:T(2,128)(2,1)} %bitcast.9, bf16[100,2,540]{2,1,0:T(2,128)(2,1)S(1)} %bitcast.6, s32[32,16]{1,0:T(8,128)S(1)} %copy.7.code_signs, s32[1,256]{1,0:T(1,128)S(1)} %bitcast.8), custom_call_target="tpu_custom_call" | custom-call | tf_op jit(solution)/shard_map/pallas_call | solution.py:388
  57.7 0.6 %copy.10 = f32[4,25,128]{2,0,1:T(4,128)} copy(f32[4,25,128]{2,0,1:T(4,128)S(1)} %bitcast.7) | data formatting | bytes 102400
Async XLA Ops:
  0.8 0.9 %copy-start = (bf16[2,100,540]{2,0,1:T(2,128)(2,1)S(1)}, bf16[2,100,540]{2,0,1:T(2,128)(2,1)}, u32[]{:S(2)}) copy-start(bf16[2,100,540]{2,0,1:T(2,128)(2,1)} %param.5) | copy-start | bytes 648004
  1.7 0.7 %copy-start.1 = (s32[256]{0:T(256)S(1)}, s32[256]{0:T(256)}, u32[]{:S(2)}) copy-start(s32[256]{0:T(256)} %param.7) | copy-start | bytes 3076

commit v4 on v3

v4 whole, which is shorter than its diff:
```python
import functools
import math

import jax
import jax.numpy as jnp
from jax import lax
from jax.experimental import pallas as pl
from jax.experimental.pallas import tpu as pltpu
from jax.sharding import PartitionSpec as P

PKT = 32
IPP_LEN = 512
LAGS = 64
NCODES = 32
NBAUD = 16
BAUD_LEN = 8
SEC_LEN = 2
GATES = 128
NSEC = 256
LANES = 128
SUBS = 4
TMS = 32
BEAMS = 25
T_DEV = 4096
GROUPS = T_DEV // LANES
ROWS = 2 * GROUPS
SPAN = 4
WEIGHT_TILES = 5
SIZES = (6, 6, 5, 4, 4)
STARTS = (0, 6, 12, 17, 21)
STEPS = len(SIZES)
MOST = max(SIZES)
BLOCK = 256
WIDE = BEAMS * LANES
BITS = 14.9
AHEAD = 2
LAG_PAIR = 4
LAG_ROUTE = 8
MESH = pl.DeviceIdType.MESH


def iota(shape, dim):
    return lax.broadcasted_iota(jnp.int32, shape, dim)


def kernel(
    streams, weights, code_signs, gate_map, out,
    held, raw_weights, raw_gates, plain, block_rows, sums, early, late, beams, signs,
    coded, skewed, row_sec, picked, gate_part, far_out, near_out,
    in_sem, w_sem, a_send, a_recv, b_send, b_recv, h_send, h_recv, z_send, z_recv, g_send, g_recv,
):
    y = lax.axis_index("sub")
    d = lax.axis_index("tm")
    z = d // 8
    core = lax.rem(d, 2)
    based = lax.rem(d + TMS - 2 * core, TMS)

    def ring(step):
        return (y, lax.rem(d + step + TMS, TMS))

    def sub_to(step):
        return (lax.rem(y + step, SUBS), d)

    def z_to(step):
        return (y, lax.rem(z + step, 4) * 8 + lax.rem(d, 8))

    def row_to(step):
        return (y, z * 8 + lax.rem(d + step, 8))

    def fetch(i):
        return pltpu.make_async_copy(streams.at[:, i], held.at[i], in_sem.at[i])

    fetch_weights = pltpu.make_async_copy(weights, raw_weights, w_sem.at[0])
    fetch_gates = pltpu.make_async_copy(gate_map, raw_gates, w_sem.at[1])
    fetch_weights.start()
    for i in range(GROUPS):
        fetch(i).start()
    fetch_gates.start()

    barrier = pltpu.get_barrier_semaphore()
    met = [sub_to(1), sub_to(3), ring(-2), ring(2)]
    met += [z_to(i) for i in (1, 2, 3)] + [row_to(i) for i in range(1, 8)]
    for device in met:
        pl.semaphore_signal(barrier, inc=1, device_id=device, device_id_type=MESH)

    channels = weights.shape[2]
    fetch_weights.wait()
    stacked = raw_weights[...].reshape(2 * weights.shape[0], channels)
    wide_rows = stacked.astype(jnp.float32)
    count = wide_rows.shape[0]
    odd = lax.rem(iota(wide_rows.shape, 0), 2) == 1
    turned_rows = jnp.where(odd, pltpu.roll(wide_rows, 1, 0), -pltpu.roll(wide_rows, count - 1, 0))
    plain[...] = jnp.zeros_like(plain)
    plain[0, :, 0:channels] = stacked
    plain[1, :, 0:channels] = turned_rows.astype(jnp.bfloat16)
    source = iota((BLOCK, BLOCK), 0)
    spread = (
        2 * lax.rem(source, LANES) + source // LANES == iota((BLOCK, BLOCK), 1)
    ).astype(jnp.bfloat16)
    for t in range(WEIGHT_TILES):
        cols = slice(t * LANES, (t + 1) * LANES)
        pair = jnp.concatenate([plain[0, :, cols], plain[1, :, cols]], 1)
        block_rows[:, t * BLOCK : (t + 1) * BLOCK] = jnp.dot(
            pair, spread, preferred_element_type=jnp.float32
        ).astype(jnp.bfloat16)
    samples = held.reshape(GROUPS, 2 * channels, LANES)

    def form(i, carry):
        for h in range(SPAN):
            fetch(SPAN * i + h).wait()
        product = jnp.dot(
            block_rows[:, 0 : 2 * channels],
            jnp.concatenate([samples[SPAN * i + h] for h in range(SPAN)], 1),
            preferred_element_type=jnp.float32,
        )
        for h in range(SPAN):
            place = SPAN * i + h
            sums[pl.ds(place, count, stride=GROUPS), :] = product[:, h * LANES : (h + 1) * LANES]
        top = jnp.max(jnp.abs(product).reshape(count // 8, 8, SPAN * LANES), axis=0)
        return jnp.maximum(carry, top)

    nothing = jnp.zeros((8, SPAN * LANES), jnp.float32)
    blocks = GROUPS // SPAN

    def level_of(top):
        most = jnp.maximum(jnp.max(top, axis=(0, 1), keepdims=True), 1e-30)
        return jnp.broadcast_to(jnp.ceil(jnp.log2(most)), (16, LANES))

    def rows_of(owner, step):
        return pl.multiple_of((owner * BEAMS + STARTS[step]) * ROWS, ROWS)

    def packed(value, power):
        steps = value.reshape(-1, 16, LANES) * jnp.exp2(BITS - power)[None]
        return jnp.round(steps).astype(jnp.int32).astype(jnp.int16).reshape(-1, LANES)

    def unpacked(ref, count):
        power = ref[count : count + 16, :].astype(jnp.int32).astype(jnp.float32)
        steps = ref[0:count, :].astype(jnp.int32).astype(jnp.float32)
        value = steps.reshape(-1, 16, LANES) * jnp.exp2(power - BITS)[None]
        return value.reshape(count, LANES), power

    def ways(way):
        return 1 if way == 0 else 3

    def send_far(step, way):
        half = SIZES[step] * GROUPS
        rows = pl.ds(STARTS[step] * GROUPS + 16 * step, half + 16)
        return pltpu.make_async_remote_copy(
            src_ref=far_out.at[way, rows],
            dst_ref=early.at[way, rows],
            send_sem=a_send.at[step, way],
            recv_sem=a_recv.at[step, way],
            device_id=sub_to(ways(way)),
            device_id_type=MESH,
        )

    def near_rows(step):
        return pl.ds(STARTS[step] * ROWS + 16 * step, SIZES[step] * ROWS + 16)

    def send_near(step, way):
        rows = near_rows(step)
        return pltpu.make_async_remote_copy(
            src_ref=near_out.at[way, rows],
            dst_ref=late.at[way, rows],
            send_sem=b_send.at[step, way],
            recv_sem=b_recv.at[step, way],
            device_id=sub_to(ways(way)),
            device_id_type=MESH,
        )

    def launch(step):
        half = SIZES[step] * GROUPS
        place = STARTS[step] * GROUPS + 16 * step
        for way in range(2):
            start = rows_of(lax.rem(y + 2, SUBS), step) + way * half
            far_out[way, place : place + half, :] = packed(sums[pl.ds(start, half), :], level)
            far_out[way, place + half : place + half + 16, :] = (
                level.astype(jnp.int32).astype(jnp.int16)
            )
            send_far(step, way).start()

    def send_edge(step, way):
        lines = pl.ds(2 * STARTS[step], 2 * SIZES[step])
        return pltpu.make_async_remote_copy(
            src_ref=beams.at[2 * core, lines],
            dst_ref=beams.at[1 if way == 0 else 2 - 2 * core, lines],
            send_sem=h_send.at[step, way],
            recv_sem=h_recv.at[step, way],
            device_id=(y, d + 1 - 2 * core) if way == 0 else ring(4 * core - 2),
            device_id_type=MESH,
        )

    row = iota((256, NCODES), 0)
    code_of = lax.rem(
        2 * lax.rem(4 * lax.rem(row, GROUPS) + row // 64, 16) + based // 16, NCODES
    )
    code_hot = (code_of == iota((256, NCODES), 1)).astype(jnp.bfloat16)
    lane16 = iota((NBAUD, LANES), 1)
    baud_hot = jnp.where(
        (lax.rem(4 * based + lane16 // BAUD_LEN, NBAUD) == iota((NBAUD, LANES), 0)) & (lane16 < 96),
        1.0,
        0.0,
    ).astype(jnp.bfloat16)
    table = (2 * code_signs[...] - 1).astype(jnp.float32).astype(jnp.bfloat16)
    by_code = lax.dot_general(
        code_hot, table, (((1,), (1,)), ((), ())), preferred_element_type=jnp.float32
    ).astype(jnp.bfloat16)
    signs[...] = jnp.dot(by_code, baud_hot, preferred_element_type=jnp.float32).astype(jnp.bfloat16)

    def relay(step):
        half = SIZES[step] * GROUPS
        place = STARTS[step] * GROUPS + 16 * step
        spot = STARTS[step] * ROWS + 16 * step
        for way in range(2):
            send_far(step, way).wait_recv()
            start = rows_of(lax.rem(y + ways(way), SUBS), step)
            passed, power = unpacked(early.at[way, pl.ds(place, half + 16)], half)
            both = jnp.maximum(power, level) + 1
            mine, rest = way * half, (1 - way) * half
            near_out[way, spot + mine : spot + mine + half, :] = packed(
                sums[pl.ds(start + mine, half), :] + passed, both
            )
            near_out[way, spot + rest : spot + rest + half, :] = packed(
                sums[pl.ds(start + rest, half), :], both
            )
            near_out[way, spot + 2 * half : spot + 2 * half + 16, :] = (
                both.astype(jnp.int32).astype(jnp.int16)
            )
            send_near(step, way).start()

    def settle(step):
        part = SIZES[step] * ROWS
        total = sums[pl.ds(rows_of(y, step), part), :]
        for way in range(2):
            send_near(step, way).wait_recv()
            total += unpacked(late.at[way, near_rows(step)], part)[0]
        beams[2 * core, 2 * STARTS[step] : 2 * (STARTS[step] + SIZES[step])] = total.astype(
            jnp.bfloat16
        ).reshape(2 * SIZES[step], GROUPS, LANES)

    def share(step):
        for way in range(2):
            send_edge(step, way).start()

    def passed_end(slot, step):
        span = SIZES[step] * ROWS
        lines = slice(2 * STARTS[step], 2 * (STARTS[step] + SIZES[step]))
        turned = pltpu.roll(beams[slot, lines].reshape(span, LANES).astype(jnp.float32), 96, 1)
        above = pltpu.roll(turned, span - 1, 0)
        last = lax.rem(iota((span, LANES), 0), GROUPS) == GROUPS - 1
        new = jnp.where(iota((span, LANES), 1) < 96, turned, jnp.where(last, 0.0, above))
        beams[slot, lines] = new.astype(jnp.bfloat16).reshape(2 * SIZES[step], GROUPS, LANES)

    def correlate(step):
        for way in range(2):
            send_edge(step, way).wait()

        @pl.when(d == 1)
        def _():
            passed_end(1, step)

        @pl.when((d == 1) | (d == TMS - 2))
        def _():
            passed_end(2, step)

        size = SIZES[step]
        span = size * ROWS
        lane = iota((span, LANES), 1)
        offset = iota((span, LANES), 0)
        lines = slice(2 * STARTS[step], 2 * (STARTS[step] + size))
        three = [beams[slot, lines].reshape(span, LANES) for slot in range(3)]
        for c in range(4):
            here, n1, n2 = [
                pltpu.roll(v, shift, 1) if shift else v
                for v, shift in ((v, (128 + 32 * (j - c)) % 128) for j, v in enumerate(three))
            ]
            mixed = jnp.where(lane < 32, here, jnp.where(lane < 64, n1, n2))
            mixed = mixed.reshape(size, ROWS, LANES) * signs[c * ROWS : (c + 1) * ROWS, :][None]
            coded[0:size, :, c] = mixed.reshape(size, 2, GROUPS, LANES)
        grams = []
        low = iota((256, LANES), 1) < 32
        for k in range(size):
            later = coded[k].reshape(256, LANES)
            turned = jnp.concatenate([-later[128:], later[:128]], 0)
            base = jnp.where(low, later, pltpu.roll(turned, 32, 1))
            gram = lax.dot_general(
                base, later, (((0,), (0,)), ((), ())), preferred_element_type=jnp.float32
            )
            real = jnp.concatenate(
                [pltpu.roll(gram[r : r + 8], 127 - r, 1) for r in (0, 8, 16, 24)], 0
            )
            imag = jnp.concatenate(
                [pltpu.roll(gram[r + 32 : r + 40], (191 - r) % 128, 1) for r in (0, 8, 16, 24)], 0
            )
            grams += [real, imag]
        gram = jnp.concatenate(grams, 0)
        for bit in (1, 2, 4):
            gram = jnp.where((offset & bit) > 0, pltpu.roll(gram, LANES - bit, 1), gram)
        gram = gram.reshape(size, 2, 32, LANES)
        skewed[0 : size * 32] = jnp.where(
            iota((size, 32, LANES), 2) < LAGS, gram[:, 0], gram[:, 1]
        ).reshape(size * 32, LANES)
        even = skewed[pl.ds(0, size * 16, stride=2), :]
        pairs = even + skewed[pl.ds(1, size * 16, stride=2), :]
        for k in range(size):
            place = (STARTS[step] + k) * LANES
            row_sec[z, :, place : place + LANES] = pairs[16 * k : 16 * k + 16].astype(
                jnp.bfloat16
            )

    def cols_of(step):
        return pl.ds(STARTS[step] * LANES, SIZES[step] * LANES)

    def send_z(step, i):
        return pltpu.make_async_remote_copy(
            src_ref=row_sec.at[z, :, cols_of(step)],
            dst_ref=row_sec.at[z, :, cols_of(step)],
            send_sem=z_send.at[step, i - 1],
            recv_sem=z_recv.at[step, i - 1],
            device_id=z_to(i),
            device_id_type=MESH,
        )

    def send_gates(step, i):
        return pltpu.make_async_remote_copy(
            src_ref=picked.at[lax.rem(d + i, 8), :, cols_of(step)],
            dst_ref=gate_part.at[i - 1, :, cols_of(step)],
            send_sem=g_send.at[step, i - 1],
            recv_sem=g_recv.at[step, i - 1],
            device_id=row_to(i),
            device_id_type=MESH,
        )

    fetch_gates.wait()
    gate_row = z * 32 + iota((32, NSEC), 0)
    named = (raw_gates[...] == gate_row).astype(jnp.bfloat16)
    col = iota((NSEC, 64), 1)
    origin = lax.rem(col // 16 * 8 + lax.rem(d, 8) + TMS - 2 * core, 16)
    section = 16 * origin + lax.rem(col, 16)
    chosen = (iota((NSEC, 64), 0) == section).astype(jnp.bfloat16)
    scale = 1.0 / math.sqrt(TMS * T_DEV / GATES)
    gate_hot = jnp.dot(named, chosen, preferred_element_type=jnp.float32).astype(jnp.bfloat16)

    def route(step):
        for i in (1, 2, 3):
            send_z(step, i).wait_recv()
        gathered = row_sec[:, :, cols_of(step)].reshape(64, SIZES[step] * LANES)
        gates = jnp.dot(gate_hot, gathered, preferred_element_type=jnp.float32) * scale
        for k in range(8):
            picked[k, :, cols_of(step)] = gates[4 * k : 4 * k + 4]
        for i in range(1, 8):
            send_gates(step, i).start()

    def finish(step):
        total = picked[lax.rem(d, 8), :, cols_of(step)]
        for i in range(1, 8):
            send_gates(step, i).wait_recv()
            total += gate_part[i - 1, :, cols_of(step)]
        out[:, cols_of(step)] = total

    level = level_of(lax.fori_loop(0, blocks, form, nothing))
    pl.semaphore_wait(barrier, len(met))
    for s in range(AHEAD):
        launch(s)
    for s in range(STEPS + LAG_ROUTE):
        if s + AHEAD < STEPS:
            launch(s + AHEAD)
        if s < STEPS:
            relay(s)
        if 1 <= s <= STEPS:
            settle(s - 1)
            share(s - 1)
        if 0 <= s - LAG_PAIR < STEPS:
            correlate(s - LAG_PAIR)
            for i in (1, 2, 3):
                send_z(s - LAG_PAIR, i).start()
        if 0 <= s - LAG_ROUTE:
            route(s - LAG_ROUTE)
    for step in range(STEPS):
        finish(step)

    for step in range(STEPS):
        for way in range(2):
            send_far(step, way).wait_send()
            send_near(step, way).wait_send()
        for i in (1, 2, 3):
            send_z(step, i).wait_send()
        for i in range(1, 8):
            send_gates(step, i).wait_send()


def body(streams, beam_weights, code_signs, gate_map):
    dma = pltpu.SemaphoreType.DMA
    channels = streams.shape[1]
    tiles = streams.reshape(2, channels, GROUPS, LANES).transpose(1, 2, 0, 3)
    paired = beam_weights.transpose(1, 0, 2)
    f32, bf16, i16 = jnp.float32, jnp.bfloat16, jnp.int16
    vmem = pl.BlockSpec(memory_space=pltpu.VMEM)
    hbm = pl.BlockSpec(memory_space=pltpu.HBM)
    summed = pl.pallas_call(
        kernel,
        out_shape=jax.ShapeDtypeStruct((4, WIDE), f32),
        in_specs=[hbm, hbm, vmem, hbm],
        out_specs=vmem,
        scratch_shapes=[
            pltpu.VMEM((GROUPS, channels, 2, LANES), bf16),
            pltpu.VMEM((100, 2, channels), bf16),
            pltpu.VMEM((1, NSEC), jnp.int32),
            pltpu.VMEM((2, 200, WEIGHT_TILES * LANES), bf16),
            pltpu.VMEM((200, WEIGHT_TILES * BLOCK), bf16),
            pltpu.VMEM((100 * ROWS, LANES), f32),
            pltpu.VMEM((2, BEAMS * GROUPS + 16 * STEPS, LANES), i16),
            pltpu.VMEM((2, BEAMS * ROWS + 16 * STEPS, LANES), i16),
            pltpu.VMEM((3, 2 * BEAMS, GROUPS, LANES), bf16),
            pltpu.VMEM((256, LANES), bf16),
            pltpu.VMEM((MOST, 2, 4, GROUPS, LANES), bf16),
            pltpu.VMEM((MOST * 32, LANES), f32),
            pltpu.VMEM((4, 16, WIDE), bf16),
            pltpu.VMEM((8, 4, WIDE), f32),
            pltpu.VMEM((7, 4, WIDE), f32),
            pltpu.VMEM((2, BEAMS * GROUPS + 16 * STEPS, LANES), i16),
            pltpu.VMEM((2, BEAMS * ROWS + 16 * STEPS, LANES), i16),
            dma((GROUPS,)), dma((2,)),
            dma((STEPS, 2)), dma((STEPS, 2)), dma((STEPS, 2)), dma((STEPS, 2)),
            dma((STEPS, 2)), dma((STEPS, 2)),
            dma((STEPS, 3)), dma((STEPS, 3)), dma((STEPS, 7)), dma((STEPS, 7)),
        ],
        compiler_params=pltpu.CompilerParams(
            collective_id=0, has_side_effects=True, vmem_limit_bytes=48 * 2**20
        ),
    )(tiles, paired, code_signs.T, gate_map.reshape(1, NSEC))
    return summed.reshape(4, BEAMS, LANES)


def solution(mesh):
    placed = (P(None, "sub", "tm"), P(None, None, "sub"), P(), P())
    return jax.shard_map(
        body, mesh=mesh, in_specs=placed, out_specs=P("tm", "sub", None), check_vma=False
    )
```

time: 58.6 us -> 49.9 us (0.85)
  Pallas kernels: 55.3 us -> 46.8 us
    pallas_call x1, Pallas kernels: 55.3 us -> 46.8 us  [body(): pl.pallas_call(kernel, out_shape=jax.ShapeDtypeStruct((4, WIDE), f32), in...]
    unnamed x6 -> x7, local copies, waits for them, and re-layouts: 3.02 us -> 2.95 us
where the time goes in v4:
time: 49.9 us; the launch traced here: 49.7 us
  Pallas kernels  46.8 us (94%)
  local copies, waits for them, and re-layouts  2.95 us (6%)
    pallas_call x1, Pallas kernels, body(): pl.pallas_call(kernel, out_shape=jax.ShapeDtypeStruct((4, WIDE), f32), in...  46.8 us
    unnamed x7, local copies, waits for them, and re-layouts  2.95 us

profile of v4, /device:TPU:1, one launch (start us, length us, event | category | flops | bytes accessed | tf_op | source)
XLA Modules:
  0.0 49.7 jit_solution(1344563034415024328)
XLA Ops:
  0.0 0.0 copy-start
  0.0 0.9 %copy-done = bf16[2,100,540]{2,0,1:T(2,128)(2,1)S(1)} copy-done((bf16[2,100,540]{2,0,1:T(2,128)(2,1)S(1)}, bf16[2,100,540]{2,0,1:T(2,128)(2,1)}, u32[]{:S(2)}) %copy-start) | copy-done | bytes 216024
  0.9 0.0 copy-start.1
  1.0 0.7 %copy-done.1 = s32[32,16]{0,1:T(8,128)S(1)} copy-done((s32[32,16]{0,1:T(8,128)S(1)}, s32[32,16]{0,1:T(8,128)}, u32[]{:S(2)}) %copy-start.1) | copy-done | bytes 2072
  1.6 0.0 copy-start.2
  1.6 0.7 %copy-done.2 = s32[256]{0:T(256)S(1)} copy-done((s32[256]{0:T(256)S(1)}, s32[256]{0:T(256)}, u32[]{:S(2)}) %copy-start.2) | copy-done | bytes 1048
  2.3 46.8 %shard_map.46 = f32[4,3200]{1,0:T(4,128)S(1)} custom-call(bf16[540,32,2,128]{3,2,1,0:T(2,128)(2,1)} %bitcast.11, bf16[100,2,540]{2,1,0:T(2,128)(2,1)S(1)} %bitcast.7, s32[16,32]{1,0:T(8,128)S(1)} %bitcast.9, s32[1,256]{1,0:T(1,128)S(1)} %bitcast.10), custom_call_target="tpu_custom_call" | custom-call | tf_op jit(solution)/shard_map/pallas_call | solution.py:400
  49.1 0.6 %copy.8 = f32[4,25,128]{2,0,1:T(4,128)} copy(f32[4,25,128]{2,0,1:T(4,128)S(1)} %bitcast.8) | data formatting | bytes 102400
Async XLA Ops:
  0.0 0.9 %copy-start = (bf16[2,100,540]{2,0,1:T(2,128)(2,1)S(1)}, bf16[2,100,540]{2,0,1:T(2,128)(2,1)}, u32[]{:S(2)}) copy-start(bf16[2,100,540]{2,0,1:T(2,128)(2,1)} %param.5) | copy-start | bytes 648004
  0.9 0.7 %copy-start.1 = (s32[32,16]{0,1:T(8,128)S(1)}, s32[32,16]{0,1:T(8,128)}, u32[]{:S(2)}) copy-start(s32[32,16]{0,1:T(8,128)} %param.6) | copy-start | bytes 6148
  1.6 0.7 %copy-start.2 = (s32[256]{0:T(256)S(1)}, s32[256]{0:T(256)}, u32[]{:S(2)}) copy-start(s32[256]{0:T(256)} %param.7) | copy-start | bytes 3076

commit v5 on v4

--- a/solution.py
+++ b/solution.py
@@ -426,7 +426,7 @@
             dma((STEPS, 3)), dma((STEPS, 3)), dma((STEPS, 7)), dma((STEPS, 7)),
         ],
         compiler_params=pltpu.CompilerParams(
-            collective_id=0, has_side_effects=True, vmem_limit_bytes=48 * 2**20
+            collective_id=0, has_side_effects=True, vmem_limit_bytes=58 * 2**20
         ),
     )(tiles, paired, code_signs.T, gate_map.reshape(1, NSEC))
     return summed.reshape(4, BEAMS, LANES)

time: 49.9 us -> 52.9 us (1.060)
  Pallas kernels: 46.8 us -> 51.3 us
  local copies, waits for them, and re-layouts: 2.95 us -> 1.43 us
    pallas_call x1, Pallas kernels: 46.8 us -> 51.3 us  [body(): pl.pallas_call(kernel, out_shape=jax.ShapeDtypeStruct((4, WIDE), f32), in...]
    unnamed x7 -> x1, local copies, waits for them, and re-layouts: 2.95 us -> 1.43 us
where the time goes in v5:
time: 52.9 us; the launch traced here: 52.7 us
  Pallas kernels  51.3 us (97%)
  local copies, waits for them, and re-layouts  1.43 us (3%)
    pallas_call x1, Pallas kernels, body(): pl.pallas_call(kernel, out_shape=jax.ShapeDtypeStruct((4, WIDE), f32), in...  51.3 us
    unnamed x1, local copies, waits for them, and re-layouts  1.43 us

profile of v5, /device:TPU:1, one launch (start us, length us, event | category | flops | bytes accessed | tf_op | source)
XLA Modules:
  0.0 52.7 jit_solution(4531400358084267116)
XLA Ops:
  0.0 51.3 %shard_map.46 = f32[4,3200]{1,0:T(4,128)} custom-call(bf16[540,32,2,128]{3,2,1,0:T(2,128)(2,1)} %bitcast.7, bf16[100,2,540]{2,1,0:T(2,128)(2,1)} %bitcast.8, s32[16,32]{1,0:T(8,128)} %bitcast.10, s32[1,256]{1,0:T(1,128)} %bitcast.11), custom_call_target="tpu_custom_call" | custom-call | tf_op jit(solution)/shard_map/pallas_call | solution.py:400
  51.3 1.4 %copy.8 = f32[4,25,128]{2,0,1:T(4,128)} copy(f32[4,25,128]{2,0,1:T(4,128)} %bitcast.9) | data formatting | bytes 102400

commit v6 on v4

--- a/solution.py
+++ b/solution.py
@@ -33,9 +33,6 @@
 BLOCK = 256
 WIDE = BEAMS * LANES
 BITS = 14.9
-AHEAD = 2
-LAG_PAIR = 4
-LAG_ROUTE = 8
 MESH = pl.DeviceIdType.MESH
 
 
@@ -360,22 +357,19 @@
 
     level = level_of(lax.fori_loop(0, blocks, form, nothing))
     pl.semaphore_wait(barrier, len(met))
-    for s in range(AHEAD):
-        launch(s)
-    for s in range(STEPS + LAG_ROUTE):
-        if s + AHEAD < STEPS:
-            launch(s + AHEAD)
-        if s < STEPS:
-            relay(s)
-        if 1 <= s <= STEPS:
-            settle(s - 1)
-            share(s - 1)
-        if 0 <= s - LAG_PAIR < STEPS:
-            correlate(s - LAG_PAIR)
-            for i in (1, 2, 3):
-                send_z(s - LAG_PAIR, i).start()
-        if 0 <= s - LAG_ROUTE:
-            route(s - LAG_ROUTE)
+    for step in range(STEPS):
+        launch(step)
+    for step in range(STEPS):
+        relay(step)
+    for step in range(STEPS):
+        settle(step)
+        share(step)
+    for step in range(STEPS):
+        correlate(step)
+        for i in (1, 2, 3):
+            send_z(step, i).start()
+    for step in range(STEPS):
+        route(step)
     for step in range(STEPS):
         finish(step)
 

time: 49.9 us -> 48.9 us (0.980)
  Pallas kernels: 46.8 us -> 45.8 us
    pallas_call x1, Pallas kernels: 46.8 us -> 45.8 us  [body(): pl.pallas_call(kernel, out_shape=jax.ShapeDtypeStruct((4, WIDE), f32), in...]
where the time goes in v6:
time: 48.9 us; the launch traced here: 48.7 us
  Pallas kernels  45.8 us (94%)
  local copies, waits for them, and re-layouts  2.95 us (6%)
    pallas_call x1, Pallas kernels, body(): pl.pallas_call(kernel, out_shape=jax.ShapeDtypeStruct((4, WIDE), f32), in...  45.8 us
    unnamed x7, local copies, waits for them, and re-layouts  2.95 us

profile of v6, /device:TPU:1, one launch (start us, length us, event | category | flops | bytes accessed | tf_op | source)
XLA Modules:
  0.0 48.7 jit_solution(12954847361213324980)
XLA Ops:
  0.0 0.0 copy-start
  0.0 0.9 %copy-done = bf16[2,100,540]{2,0,1:T(2,128)(2,1)S(1)} copy-done((bf16[2,100,540]{2,0,1:T(2,128)(2,1)S(1)}, bf16[2,100,540]{2,0,1:T(2,128)(2,1)}, u32[]{:S(2)}) %copy-start) | copy-done | bytes 216024
  0.9 0.0 copy-start.1
  1.0 0.7 %copy-done.1 = s32[32,16]{0,1:T(8,128)S(1)} copy-done((s32[32,16]{0,1:T(8,128)S(1)}, s32[32,16]{0,1:T(8,128)}, u32[]{:S(2)}) %copy-start.1) | copy-done | bytes 2072
  1.6 0.0 copy-start.2
  1.6 0.7 %copy-done.2 = s32[256]{0:T(256)S(1)} copy-done((s32[256]{0:T(256)S(1)}, s32[256]{0:T(256)}, u32[]{:S(2)}) %copy-start.2) | copy-done | bytes 1048
  2.3 45.8 %shard_map.46 = f32[4,3200]{1,0:T(4,128)S(1)} custom-call(bf16[540,32,2,128]{3,2,1,0:T(2,128)(2,1)} %bitcast.11, bf16[100,2,540]{2,1,0:T(2,128)(2,1)S(1)} %bitcast.7, s32[16,32]{1,0:T(8,128)S(1)} %bitcast.9, s32[1,256]{1,0:T(1,128)S(1)} %bitcast.10), custom_call_target="tpu_custom_call" | custom-call | tf_op jit(solution)/shard_map/pallas_call | solution.py:394
  48.1 0.6 %copy.8 = f32[4,25,128]{2,0,1:T(4,128)} copy(f32[4,25,128]{2,0,1:T(4,128)S(1)} %bitcast.8) | data formatting | bytes 102400
Async XLA Ops:
  0.0 0.9 %copy-start = (bf16[2,100,540]{2,0,1:T(2,128)(2,1)S(1)}, bf16[2,100,540]{2,0,1:T(2,128)(2,1)}, u32[]{:S(2)}) copy-start(bf16[2,100,540]{2,0,1:T(2,128)(2,1)} %param.5) | copy-start | bytes 648004
  0.9 0.7 %copy-start.1 = (s32[32,16]{0,1:T(8,128)S(1)}, s32[32,16]{0,1:T(8,128)}, u32[]{:S(2)}) copy-start(s32[32,16]{0,1:T(8,128)} %param.6) | copy-start | bytes 6148
  1.6 0.7 %copy-start.2 = (s32[256]{0:T(256)S(1)}, s32[256]{0:T(256)}, u32[]{:S(2)}) copy-start(s32[256]{0:T(256)} %param.7) | copy-start | bytes 3076

commit v7 on v6

--- a/solution.py
+++ b/solution.py
@@ -361,13 +361,14 @@
         launch(step)
     for step in range(STEPS):
         relay(step)
-    for step in range(STEPS):
-        settle(step)
-        share(step)
-    for step in range(STEPS):
-        correlate(step)
-        for i in (1, 2, 3):
-            send_z(step, i).start()
+    for step in range(STEPS + 2):
+        if step < STEPS:
+            settle(step)
+            share(step)
+        if step >= 2:
+            correlate(step - 2)
+            for i in (1, 2, 3):
+                send_z(step - 2, i).start()
     for step in range(STEPS):
         route(step)
     for step in range(STEPS):

time: 48.9 us -> 49.4 us (1.010)
  Pallas kernels: 45.8 us -> 46.3 us
    pallas_call x1, Pallas kernels: 45.8 us -> 46.3 us  [body(): pl.pallas_call(kernel, out_shape=jax.ShapeDtypeStruct((4, WIDE), f32), in...]
where the time goes in v7:
time: 49.4 us; the launch traced here: 49.2 us
  Pallas kernels  46.3 us (94%)
  local copies, waits for them, and re-layouts  2.95 us (6%)
    pallas_call x1, Pallas kernels, body(): pl.pallas_call(kernel, out_shape=jax.ShapeDtypeStruct((4, WIDE), f32), in...  46.3 us
    unnamed x7, local copies, waits for them, and re-layouts  2.95 us

profile of v7, /device:TPU:1, one launch (start us, length us, event | category | flops | bytes accessed | tf_op | source)
XLA Modules:
  0.0 49.2 jit_solution(10294447553083837789)
XLA Ops:
  0.0 0.0 copy-start
  0.0 0.9 %copy-done = bf16[2,100,540]{2,0,1:T(2,128)(2,1)S(1)} copy-done((bf16[2,100,540]{2,0,1:T(2,128)(2,1)S(1)}, bf16[2,100,540]{2,0,1:T(2,128)(2,1)}, u32[]{:S(2)}) %copy-start) | copy-done | bytes 216024
  0.9 0.0 copy-start.1
  1.0 0.7 %copy-done.1 = s32[32,16]{0,1:T(8,128)S(1)} copy-done((s32[32,16]{0,1:T(8,128)S(1)}, s32[32,16]{0,1:T(8,128)}, u32[]{:S(2)}) %copy-start.1) | copy-done | bytes 2072
  1.6 0.0 copy-start.2
  1.6 0.7 %copy-done.2 = s32[256]{0:T(256)S(1)} copy-done((s32[256]{0:T(256)S(1)}, s32[256]{0:T(256)}, u32[]{:S(2)}) %copy-start.2) | copy-done | bytes 1048
  2.3 46.3 %shard_map.46 = f32[4,3200]{1,0:T(4,128)S(1)} custom-call(bf16[540,32,2,128]{3,2,1,0:T(2,128)(2,1)} %bitcast.11, bf16[100,2,540]{2,1,0:T(2,128)(2,1)S(1)} %bitcast.7, s32[16,32]{1,0:T(8,128)S(1)} %bitcast.9, s32[1,256]{1,0:T(1,128)S(1)} %bitcast.10), custom_call_target="tpu_custom_call" | custom-call | tf_op jit(solution)/shard_map/pallas_call | solution.py:395
  48.6 0.6 %copy.8 = f32[4,25,128]{2,0,1:T(4,128)} copy(f32[4,25,128]{2,0,1:T(4,128)S(1)} %bitcast.8) | data formatting | bytes 102400
Async XLA Ops:
  0.0 0.9 %copy-start = (bf16[2,100,540]{2,0,1:T(2,128)(2,1)S(1)}, bf16[2,100,540]{2,0,1:T(2,128)(2,1)}, u32[]{:S(2)}) copy-start(bf16[2,100,540]{2,0,1:T(2,128)(2,1)} %param.5) | copy-start | bytes 648004
  0.9 0.7 %copy-start.1 = (s32[32,16]{0,1:T(8,128)S(1)}, s32[32,16]{0,1:T(8,128)}, u32[]{:S(2)}) copy-start(s32[32,16]{0,1:T(8,128)} %param.6) | copy-start | bytes 6148
  1.6 0.7 %copy-start.2 = (s32[256]{0:T(256)S(1)}, s32[256]{0:T(256)}, u32[]{:S(2)}) copy-start(s32[256]{0:T(256)} %param.7) | copy-start | bytes 3076

commit v8 on v6

--- a/solution.py
+++ b/solution.py
@@ -26,8 +26,8 @@
 ROWS = 2 * GROUPS
 SPAN = 4
 WEIGHT_TILES = 5
-SIZES = (6, 6, 5, 4, 4)
-STARTS = (0, 6, 12, 17, 21)
+SIZES = (4, 4, 4, 4, 3, 3, 3)
+STARTS = (0, 4, 8, 12, 16, 19, 22)
 STEPS = len(SIZES)
 MOST = max(SIZES)
 BLOCK = 256

time: 48.9 us -> 50.5 us (1.033)
  Pallas kernels: 45.8 us -> 47.3 us
    pallas_call x1, Pallas kernels: 45.8 us -> 47.3 us  [body(): pl.pallas_call(kernel, out_shape=jax.ShapeDtypeStruct((4, WIDE), f32), in...]
where the time goes in v8:
time: 50.5 us; the launch traced here: 50.3 us
  Pallas kernels  47.3 us (94%)
  local copies, waits for them, and re-layouts  2.95 us (6%)
    pallas_call x1, Pallas kernels, body(): pl.pallas_call(kernel, out_shape=jax.ShapeDtypeStruct((4, WIDE), f32), in...  47.3 us
    unnamed x7, local copies, waits for them, and re-layouts  2.95 us

profile of v8, /device:TPU:1, one launch (start us, length us, event | category | flops | bytes accessed | tf_op | source)
XLA Modules:
  0.0 50.3 jit_solution(12295508549396334857)
XLA Ops:
  0.0 0.0 copy-start
  0.0 0.9 %copy-done = bf16[2,100,540]{2,0,1:T(2,128)(2,1)S(1)} copy-done((bf16[2,100,540]{2,0,1:T(2,128)(2,1)S(1)}, bf16[2,100,540]{2,0,1:T(2,128)(2,1)}, u32[]{:S(2)}) %copy-start) | copy-done | bytes 216024
  0.9 0.0 copy-start.1
  1.0 0.7 %copy-done.1 = s32[32,16]{0,1:T(8,128)S(1)} copy-done((s32[32,16]{0,1:T(8,128)S(1)}, s32[32,16]{0,1:T(8,128)}, u32[]{:S(2)}) %copy-start.1) | copy-done | bytes 2072
  1.6 0.0 copy-start.2
  1.6 0.7 %copy-done.2 = s32[256]{0:T(256)S(1)} copy-done((s32[256]{0:T(256)S(1)}, s32[256]{0:T(256)}, u32[]{:S(2)}) %copy-start.2) | copy-done | bytes 1048
  2.3 47.3 %shard_map.46 = f32[4,3200]{1,0:T(4,128)S(1)} custom-call(bf16[540,32,2,128]{3,2,1,0:T(2,128)(2,1)} %bitcast.11, bf16[100,2,540]{2,1,0:T(2,128)(2,1)S(1)} %bitcast.7, s32[16,32]{1,0:T(8,128)S(1)} %bitcast.9, s32[1,256]{1,0:T(1,128)S(1)} %bitcast.10), custom_call_target="tpu_custom_call" | custom-call | tf_op jit(solution)/shard_map/pallas_call | solution.py:394
  49.7 0.6 %copy.8 = f32[4,25,128]{2,0,1:T(4,128)} copy(f32[4,25,128]{2,0,1:T(4,128)S(1)} %bitcast.8) | data formatting | bytes 102400
Async XLA Ops:
  0.0 0.9 %copy-start = (bf16[2,100,540]{2,0,1:T(2,128)(2,1)S(1)}, bf16[2,100,540]{2,0,1:T(2,128)(2,1)}, u32[]{:S(2)}) copy-start(bf16[2,100,540]{2,0,1:T(2,128)(2,1)} %param.5) | copy-start | bytes 648004
  0.9 0.7 %copy-start.1 = (s32[32,16]{0,1:T(8,128)S(1)}, s32[32,16]{0,1:T(8,128)}, u32[]{:S(2)}) copy-start(s32[32,16]{0,1:T(8,128)} %param.6) | copy-start | bytes 6148
  1.6 0.7 %copy-start.2 = (s32[256]{0:T(256)S(1)}, s32[256]{0:T(256)}, u32[]{:S(2)}) copy-start(s32[256]{0:T(256)} %param.7) | copy-start | bytes 3076
